TPU v7x, 128 devices: a whole 4x4x4 slice. The times are simulated.
128 devices in a mesh: gx: 16 (over y, x), gy: 8 (over z, core).
Axes of the slice: x: 4, y: 4, z: 4, core: 2. Of those that a mesh axis runs over, the one named last changes fastest.
Arguments:
- adjoint: float32 [40, 16, 128, 1024], P(None, None, 'gx', 'gy'), may hold values from -6 to 6
- concentration: float32 [40, 16, 128, 1024], P(None, None, 'gx', 'gy'), may hold values from 0.1 to 2
- courant_x: float32 [16, 128, 1024], P(None, 'gx', 'gy'), may hold values from -0.3 to 0.3
- courant_y: float32 [16, 128, 1024], P(None, 'gx', 'gy'), may hold values from -0.3 to 0.3
- diffusion: float32 [16], replicated, may hold values from 0.02 to 0.1
- coag_kernel: float32 [40, 40], replicated, may hold values from 0.005 to 0.03
- pixel_column: int32 [262144], P(('gx', 'gy')), may hold values from 0 to 1023
- pixel_owner: int32 [262144, 1], P(('gx', 'gy')), may hold values from 0 to 127; in each aligned block of 2048 rows (0 to 2047, 2048 to 4095, ...) at most 64 rows name the same one
- pixel_slot: int32 [262144], P(('gx', 'gy')), may hold values from 0 to 127
- pixel_level: int32 [262144], P(('gx', 'gy')), may hold values from 0 to 15
- pixel_weight: float32 [262144], P(('gx', 'gy')), may hold values from 0.2 to 1
Outputs:
- adjoint_next: float32 [40, 16, 128, 1024], P(None, None, 'gx', 'gy')
- emission_gradient: float32 [40, 16384], P(None, ('gx', 'gy'))
Inputs may be any that keep to these rules, and one draw needn't show every extreme that they name: `pixel_column`: column a * 128 + b is the column a along the east-west and b along the north-south dimension of the tile of the device that holds the row. `pixel_owner`: among the rows of one device, no owner appears more than 64 times.
All inputs are finite; a program needn't handle non-finite values.
Results may differ from a plain program's by a relative error of at most 0.000076.
Values sent between devices are 32-bit elements; how exact they have to be, the bound alone decides.
A program may use at most 128 MiB of HBM per device.

v0:
```python
import jax
import jax.numpy as jnp
from jax import lax
from jax.sharding import PartitionSpec as P

DET_DEV = 128


def extended(shard, sides, width):
    for axis, dim in sides:
        size, length = (lax.axis_size(axis), shard.shape[dim])
        up = [(i, (i + 1) % size) for i in range(size - 1)]
        down = [(j, i) for i, j in up]
        last = lax.slice_in_dim(shard, length - width, length, axis=dim)
        leading = lax.slice_in_dim(shard, 0, width, axis=dim)
        before = lax.ppermute(last, axis, up)
        after = lax.ppermute(leading, axis, down)
        shard = jnp.concatenate([before, shard, after], axis=dim)
    return shard


def transport(lam_pad, cx_pad, cy_pad, kappa_lev):
    centre = lam_pad[..., 1:-1, 1:-1]
    east = lam_pad[..., 2:, 1:-1]
    west = lam_pad[..., :-2, 1:-1]
    north = lam_pad[..., 1:-1, 2:]
    south = lam_pad[..., 1:-1, :-2]
    keep = (
        1.0 - jnp.abs(cx_pad[..., 1:-1, 1:-1]) - jnp.abs(cy_pad[..., 1:-1, 1:-1]) - 4.0 * kappa_lev
    )
    moved = keep * centre
    moved = moved + jnp.maximum(cx_pad[..., 2:, 1:-1], 0.0) * east
    moved = moved + jnp.maximum(-cx_pad[..., :-2, 1:-1], 0.0) * west
    moved = moved + jnp.maximum(cy_pad[..., 1:-1, 2:], 0.0) * north
    moved = moved + jnp.maximum(-cy_pad[..., 1:-1, :-2], 0.0) * south
    return moved + kappa_lev * (east + west + north + south)


def coagulate(moved, concentration, coag_kernel):
    sections = moved.shape[0]
    flat_lam = moved.reshape(sections, -1)
    flat_conc = concentration.reshape(sections, -1)
    rate = jnp.dot(
        coag_kernel, flat_conc, precision=lax.Precision.HIGHEST, preferred_element_type=jnp.float32
    )
    upper = jnp.concatenate([flat_lam[1:], jnp.zeros_like(flat_lam[:1])], axis=0) - flat_lam
    back = jnp.dot(
        coag_kernel.T,
        upper * flat_conc,
        precision=lax.Precision.HIGHEST,
        preferred_element_type=jnp.float32,
    )
    return (flat_lam + upper * rate + back).reshape(moved.shape)


def plume_profile(level_ids, levels):
    heights = jnp.arange(levels, dtype=jnp.float32)[:, None] - level_ids[None, :].astype(
        jnp.float32
    )
    weights = jnp.exp(-heights * heights / 8.0)
    return weights / jnp.sum(weights, axis=0, keepdims=True)


def per_device(
    adjoint,
    concentration,
    courant_x,
    courant_y,
    diffusion,
    coag_kernel,
    pixel_column,
    pixel_owner,
    pixel_slot,
    pixel_level,
    pixel_weight,
):
    sections = adjoint.shape[0]
    levels = adjoint.shape[1]
    stacked = jnp.concatenate([adjoint, courant_x[None], courant_y[None]], axis=0)
    padded = extended(stacked, (("gx", 2), ("gy", 3)), 1)
    kappa_lev = diffusion[:, None, None]
    moved = transport(padded[:sections], padded[sections], padded[sections + 1], kappa_lev)
    adjoint_next = coagulate(moved, concentration, coag_kernel)
    columns = adjoint_next.reshape(sections, levels, -1)
    picked = jnp.take(columns, pixel_column, axis=2)
    profile = plume_profile(pixel_level, levels)
    contrib = (
        jnp.einsum("klp,lp->kp", picked, profile, precision=lax.Precision.HIGHEST)
        * pixel_weight[None, :]
    )
    peer_count = lax.axis_size(("gx", "gy"))
    det_count = DET_DEV
    owner_ids = pixel_owner[:, 0]
    target = owner_ids * det_count + pixel_slot
    totals = jnp.zeros((sections, peer_count * det_count), jnp.float32).at[:, target].add(contrib)
    gradient = lax.psum_scatter(totals, ("gx", "gy"), scatter_dimension=1, tiled=True)
    return (adjoint_next, gradient)


def solution(mesh):
    placed = (
        P(None, None, "gx", "gy"),
        P(None, None, "gx", "gy"),
        P(None, "gx", "gy"),
        P(None, "gx", "gy"),
        P(),
        P(),
        P(("gx", "gy")),
        P(("gx", "gy"), None),
        P(("gx", "gy")),
        P(("gx", "gy")),
        P(("gx", "gy")),
    )
    return jax.shard_map(
        per_device,
        mesh=mesh,
        in_specs=placed,
        out_specs=(P(None, None, "gx", "gy"), P(None, ("gx", "gy"))),
        check_vma=False,
    )
```

profile of v0, /device:TPU:0, one launch (start us, length us, event | category | flops | bytes accessed | tf_op | source)
XLA Modules:
  0.0 814.5 jit_solution(7808468027584249508)
XLA Ops:
  7.2 0.0 copy-start
  7.2 0.0 reduce-scatter.2.cloned.1.call-start
  7.2 2.3 copy.32
  9.6 0.0 copy-start.7
  9.6 0.0 copy-start.9
  9.6 0.0 copy-start.10
  9.6 0.0 copy-start.8
  9.7 3.5 collective-permute-start
  13.2 1.3 collective-permute-start.1
  14.6 0.1 fusion.17
  14.7 0.6 compare_select_fusion.1
  15.3 0.7 divide_bitcast_fusion
  16.0 4.5 collective-permute-done
  20.5 4.1 collective-permute-done.1
  24.6 0.2 pad_maximum_fusion
  24.8 4.0 fusion.26
  28.8 3.0 copy.33
  31.8 1.9 collective-permute-start.2
  33.8 3.6 copy.34
  37.4 1.3 collective-permute-start.3
  38.6 1.2 broadcast_multiply_fusion.1
  39.8 3.2 copy.44
  43.0 3.7 copy.35
  46.7 3.6 copy.36
  50.3 1.4 maximum_bitcast_fusion
  51.7 0.2 fusion.21
  51.8 0.6 copy-done.2
  52.4 1.0 copy-done.3
  53.5 7.2 multiply_add_fusion
  60.7 0.2 slice.97
  60.9 1.1 copy.40
  62.1 1.1 copy.69
  63.2 0.2 pad.77
  63.4 0.0 copy-start.4
  63.4 1.5 copy.47
  64.9 0.2 copy-done.4
  65.2 5.3 fusion.1
  70.5 6.5 fusion
  77.0 3.0 copy.50
  80.0 7.9 copy.42
  87.9 22.2 %gather_fusion = f32[2048,40,16]{1,2,0:T(8,128)} fusion(f32[40,16,1024]{0,1,2:T(8,128)} %copy.42, s32[2048]{0:T(1024)S(1)} %fusion.23), kind=kCustom, calls=%fused_computation | custom fusion | bytes 10493952 | tf_op jit(solution)/shard_map/jit(_take)/gather | solution.py:85
  110.1 22.2 %fusion.2 = f32[2048,1,40]{2,1,0:T(1,128)} fusion(f32[16,2048,1]{0,2,1:T(1,128)} %copy.44, f32[2048,40,16]{1,2,0:T(8,128)} %gather_fusion, pred[2048]{0:T(1024)(128)(4,1)S(1)} %compare_and_fusion), kind=kOutput, calls=%fused_computation.6 | convolution fusion | flops 17039360 | bytes 5703680 | tf_op jit(solution)/shard_map/klp,lp->kp/dot_general | solution.py:88
  132.4 16.9 %scatter_custom_fusion = f32[40,16384]{0,1:T(8,128)} fusion(s32[2048]{0:T(1024)} %compare_select_fusion.1, f32[]{:T(128)} %constant.12.clone.1, f32[2048,40]{1,0:T(8,128)} %bitcast.62, f32[2048]{0:T(1024)S(1)} %copy-done.11), kind=kCustom, calls=%fused_computation.11 | custom fusion | flops 163840 | bytes 3678720 | tf_op jit(solution)/shard_map/scatter-add | solution.py:95
  149.2 0.0 reduce-scatter.2.cloned.1.call-update
  149.3 0.0 copy-start.1
  149.3 2.0 copy.49
  151.2 654.9 %reduce-scatter.2.cloned.1.call-done = f32[40,128]{0,1:T(8,128)} async-done(((f32[40,16384]{0,1:T(8,128)}), f32[40,128]{0,1:T(8,128)}) %reduce-scatter.2.cloned.1.call-update) | async-done | bytes 20496 | tf_op jit(solution)/shard_map/reduce_scatter | solution.py:96
  806.2 1.5 copy.43
  (26 shorter events, 0.1 us)
Async XLA Ops:
  7.2 57.8 %copy-start = (f32[40,40]{1,0:T(8,128)S(1)}, f32[40,40]{1,0:T(8,128)}, u32[]{:S(2)}) copy-start(f32[40,40]{1,0:T(8,128)} %param.16) | copy-start | bytes 19204
  7.2 2.4 copy-start.6
  7.2 2.4 copy-start.5
  7.2 799.0 %reduce-scatter.2.cloned.1.call-start = ((), (), s32[]{:S(2)}) async-start(), calls=%async_computation.1 | async-start | bytes 8454144 | tf_op jit(solution)/shard_map/reduce_scatter | solution.py:96
  9.6 4.9 copy-start.7
  9.6 5.0 copy-start.9
  9.6 5.0 copy-start.10
  9.6 5.1 copy-start.8
  9.7 10.8 %collective-permute-start = (f32[42,16,1,128]{3,1,2,0:T(8,128)S(1)}, f32[42,16,1,128]{3,1,2,0:T(8,128)S(1)}, u32[]{:S(2)}, u32[]{:S(2)}) collective-permute-start(f32[42,16,1,128]{3,1,2,0:T(8,128)S(1)} %get-tuple-element.14), channel_id=1, source_target_pairs={{0,8},{8,16},{16,24},{24,32},{32,40},{40,48},{48,56},{56,64},{64,7... | collective-permute-start | bytes 1032200 | tf_op jit(solution)/shard_map/ppermute | solution.py:16
  13.2 11.4 %collective-permute-start.1 = (f32[42,16,1,128]{3,1,2,0:T(8,128)S(1)}, f32[42,16,1,128]{3,1,2,0:T(8,128)S(1)}, u32[]{:S(2)}, u32[]{:S(2)}) collective-permute-start(f32[42,16,1,128]{3,1,2,0:T(8,128)S(1)} %get-tuple-element.15), channel_id=1, source_target_pairs={{8,0},{16,8},{24,16},{32,24},{40,32},{48,40},{56,48},{64,56},{72,6... | collective-permute-start | bytes 1032200 | tf_op jit(solution)/shard_map/ppermute | solution.py:17
  31.8 11.2 %collective-permute-start.2 = (f32[42,16,10,1]{0,1,3,2:T(8,128)S(1)}, f32[42,16,10,1]{0,1,3,2:T(8,128)}, u32[]{:S(2)}, u32[]{:S(2)}) collective-permute-start(f32[42,16,10,1]{0,1,3,2:T(8,128)S(1)} %copy.33), channel_id=1, source_target_pairs={{0,1},{1,2},{2,3},{3,4},{4,5},{5,6},{6,7},{8,9},{9,10},{10,11},{11... | collective-permute-start | bytes 80648 | tf_op jit(solution)/shard_map/ppermute | solution.py:16
  37.4 9.3 %collective-permute-start.3 = (f32[42,16,10,1]{0,1,3,2:T(8,128)}, f32[42,16,10,1]{0,1,3,2:T(8,128)}, u32[]{:S(2)}, u32[]{:S(2)}) collective-permute-start(f32[42,16,10,1]{0,1,3,2:T(8,128)} %copy.34), channel_id=1, source_target_pairs={{1,0},{2,1},{3,2},{4,3},{5,4},{6,5},{7,6},{9,8},{10,9},{11,10},{12... | collective-permute-start | bytes 80648 | tf_op jit(solution)/shard_map/ppermute | solution.py:17
  50.3 1.4 copy-start.13
  50.3 2.1 copy-start.2
  50.3 3.2 copy-start.3
  50.3 3.2 copy-start.12
  63.4 1.7 copy-start.4
  110.1 22.2 %copy-start.11 = (f32[2048]{0:T(1024)S(1)}, f32[2048]{0:T(1024)}, u32[]{:S(2)}) copy-start(f32[2048]{0:T(1024)} %param.21) | copy-start | bytes 24580
  149.3 658.4 %copy-start.1 = (f32[40,40]{1,0:T(8,128)S(1)}, f32[40,40]{1,0:T(8,128)}, u32[]{:S(2)}) copy-start(f32[40,40]{1,0:T(8,128)} %param.16) | copy-start | bytes 19204
Sparse Core Ops, SparseCore 0:
  149.4 656.7 reduce-scatter.1
where the time goes:
time: 815 us
  waiting for transfers between devices  664 us (81%)
  local copies, waits for them, and re-layouts  66.1 us (8%)
  matrix products  34 us (4%)
  other arithmetic  28.4 us (3%)
  between operations  14.3 us (2%)
    reduce_scatter x1, waiting for transfers between devices, per_device(): lax.psum_scatter(totals, ('gx', 'gy'), scatter_dimension=1, tiled=True)  655 us
    gather x1, local copies, waits for them, and re-layouts, per_device(): picked = jnp.take(columns, pixel_column, axis=2)  22.2 us
    dot_general x1, matrix products, per_device(): jnp.einsum('klp,lp->kp', picked, profile, precision=lax.Precision.HIGHEST)  22.2 us
    scatter-add x1, other arithmetic, per_device(): jnp.zeros((sections, peer_count * det_count), jnp.float32).at[:, target]  16.9 us
  transfers between devices with their start and end apart: 5, of which 3 were waited for; matrix products, arithmetic and copies ran while one was open for 2% of the time, Pallas kernels for 0%

commit v1 on v0

v1 whole, which is shorter than its diff:
```python
import jax
import jax.numpy as jnp
from jax import lax
from jax.experimental import pallas as pl
from jax.experimental.pallas import tpu as pltpu
from jax.sharding import PartitionSpec as P

MESH = pl.DeviceIdType.MESH
F32 = jnp.float32
BF16 = jnp.bfloat16
SEC, LEV, CX, CY = 40, 16, 8, 128
PIX = 2048
LCH = 4
TILE = 256
BANDS = ((0, 16), (16, 16), (32, 8))


def split(v):
    hi = v.astype(BF16).astype(F32)
    return hi, v - hi


def place():
    gx = lax.axis_index("gx")
    gy = lax.axis_index("gy")
    return lax.rem(gx, 4), gx // 4, gy // 2, lax.rem(gy, 2)


def halo_kernel(kap_ref, adj_ref, cx_ref, cy_ref, out_x, out_y, px, py, rx, ry, ssem, rsem):
    gx = lax.axis_index("gx")
    gy = lax.axis_index("gy")
    peers = (
        (lax.rem(gx + 15, 16), gy),
        (lax.rem(gx + 1, 16), gy),
        (gx, lax.rem(gy + 7, 8)),
        (gx, lax.rem(gy + 1, 8)),
    )
    barrier = pltpu.get_barrier_semaphore()
    for peer in peers:
        pl.semaphore_signal(barrier, 1, device_id=peer, device_id_type=MESH)
    kap = kap_ref[...]
    first = jnp.maximum(cx_ref[:, 0, :], 0.0) + kap
    last = jnp.maximum(-cx_ref[:, CX - 1, :], 0.0) + kap

    def fill(k, c):
        px[0, k] = adj_ref[k, :, 0, :] * first
        px[1, k] = adj_ref[k, :, CX - 1, :] * last
        return c

    lax.fori_loop(0, SEC, fill, 0)
    pl.semaphore_wait(barrier, 4)
    copies = [
        pltpu.make_async_remote_copy(
            px.at[i], rx.at[i], ssem.at[i], rsem.at[i], device_id=peers[i], device_id_type=MESH
        )
        for i in range(2)
    ]
    for c in copies:
        c.start()
    lane = lax.broadcasted_iota(jnp.int32, (SEC, CY), 1)

    def edge(l, carry):
        low, high = carry
        for x in range(CX):
            a = adj_ref[:, l, x, :]
            cyr = cy_ref[l, pl.ds(x, 1), :]
            kp = kap_ref[pl.ds(l, 1), :]
            q = l * CX + x
            s = pltpu.roll(a * (jnp.maximum(cyr, 0.0) + kp), q, 1)
            n = pltpu.roll(a * (jnp.maximum(-cyr, 0.0) + kp), q + 1, 1)
            low = jnp.where(lane == q, s, low)
            high = jnp.where(lane == q, n, high)
        return low, high

    zero = jnp.zeros((SEC, CY), F32)
    low, high = lax.fori_loop(0, LEV, edge, (zero, zero))
    py[0] = low
    py[1] = high
    more = [
        pltpu.make_async_remote_copy(
            py.at[i],
            ry.at[i],
            ssem.at[2 + i],
            rsem.at[2 + i],
            device_id=peers[2 + i],
            device_id_type=MESH,
        )
        for i in range(2)
    ]
    for c in more:
        c.start()
    for c in more:
        c.wait()
    out_y[0] = jnp.where(gy == 7, 0.0, ry[0])
    out_y[1] = jnp.where(gy == 0, 0.0, ry[1])
    for c in copies:
        c.wait()
    out_x[0] = jnp.where(gx == 15, 0.0, rx[0])
    out_x[1] = jnp.where(gx == 0, 0.0, rx[1])


def halos(kap, adjoint, courant_x, courant_y):
    vmem = pl.BlockSpec(memory_space=pltpu.VMEM)
    return pl.pallas_call(
        halo_kernel,
        out_shape=(
            jax.ShapeDtypeStruct((2, SEC, LEV, CY), F32),
            jax.ShapeDtypeStruct((2, SEC, CY), F32),
        ),
        in_specs=[vmem] * 4,
        out_specs=(vmem, vmem),
        scratch_shapes=[
            pltpu.VMEM((2, SEC, LEV, CY), F32),
            pltpu.VMEM((2, SEC, CY), F32),
            pltpu.VMEM((2, SEC, LEV, CY), F32),
            pltpu.VMEM((2, SEC, CY), F32),
            pltpu.SemaphoreType.DMA((4,)),
            pltpu.SemaphoreType.DMA((4,)),
        ],
        compiler_params=pltpu.CompilerParams(
            collective_id=0, has_side_effects=True, vmem_limit_bytes=48 << 20
        ),
    )(kap, adjoint, courant_x, courant_y)


def local_kernel(
    kap_ref, adj_ref, conc_ref, cx_ref, cy_ref, hx_ref, hy_ref, ker_ref, kert_ref,
    pix_ref, wgt_ref, out_ref, dense_ref, held, contrib,
):
    l = pl.program_id(0)
    lane = lax.broadcasted_iota(jnp.int32, (SEC, CY), 1)
    row = lax.broadcasted_iota(jnp.int32, (SEC, CY), 0)
    kap = kap_ref[pl.ds(l, 1), :]
    hn = pltpu.roll(hy_ref[0], lax.rem(CY - l * CX, CY), 1)
    hs = pltpu.roll(hy_ref[1], lax.rem(CY - l * CX, CY), 1)
    adj = [adj_ref[:, 0, x, :] for x in range(CX)]
    cxr = [cx_ref[0, pl.ds(x, 1), :] for x in range(CX)]
    moved, ups, concs = [], [], []
    for x in range(CX):
        cyr = cy_ref[0, pl.ds(x, 1), :]
        a = adj[x]
        m = (1.0 - jnp.abs(cxr[x]) - jnp.abs(cyr) - 4.0 * kap) * a
        if x < CX - 1:
            m = m + (jnp.maximum(cxr[x + 1], 0.0) + kap) * adj[x + 1]
        else:
            m = m + hx_ref[0, :, l, :]
        if x > 0:
            m = m + (jnp.maximum(-cxr[x - 1], 0.0) + kap) * adj[x - 1]
        else:
            m = m + hx_ref[1, :, l, :]
        north = (jnp.maximum(cyr, 0.0) + kap) * a
        south = (jnp.maximum(-cyr, 0.0) + kap) * a
        nh = pltpu.roll(hn, (CY - x) % CY, 1)
        sh = pltpu.roll(hs, (CY - 1 - x) % CY, 1)
        m = m + pltpu.roll(jnp.where(lane == 0, nh, north), CY - 1, 1)
        m = m + pltpu.roll(jnp.where(lane == CY - 1, sh, south), 1, 1)
        nxt = jnp.where(row == SEC - 1, 0.0, pltpu.roll(m, SEC - 1, 0))
        moved.append(m)
        ups.append(nxt - m)
        concs.append(conc_ref[:, 0, x, :])
    m = jnp.concatenate(moved, axis=1)
    up = jnp.concatenate(ups, axis=1)
    cc = jnp.concatenate(concs, axis=1)

    def product(k, v):
        kh, kl = split(k)
        vh, vl = split(v)
        k3 = jnp.concatenate([kh, kh, kl], axis=1).astype(BF16)
        v3 = jnp.concatenate([vh, vl, vh], axis=0).astype(BF16)
        return jnp.dot(k3, v3, preferred_element_type=F32)

    rate = product(ker_ref[...], cc)
    back = product(kert_ref[...], up * cc)
    res = m + up * rate + back
    for x in range(CX):
        out_ref[:, 0, x, :] = res[:, x * CY:(x + 1) * CY]
    rh, rl = split(res)
    held[l] = jnp.concatenate([rh, rl], axis=0).astype(BF16)

    @pl.when(l == LEV - 1)
    def _():
        cells = lax.broadcasted_iota(jnp.int32, (CX * CY, TILE), 0)

        def gather(t, c):
            at = pl.ds(pl.multiple_of(t * TILE, TILE), TILE)
            onehot = jnp.where(cells == pix_ref[pl.ds(0, 1), at], 1.0, 0.0).astype(BF16)
            plev = pix_ref[pl.ds(1, 1), at].astype(F32)
            height = lax.broadcasted_iota(jnp.int32, (LEV, TILE), 0).astype(F32) - plev
            prof = jnp.exp(-height * height / 8.0)
            prof = prof / jnp.sum(prof, axis=0, keepdims=True) * wgt_ref[:, at]
            total = jnp.zeros((SEC, TILE), F32)
            for j in range(LEV // LCH):
                block = held[pl.ds(j * LCH, LCH)].reshape(LCH * 2 * SEC, CX * CY)
                got = jnp.dot(block, onehot, preferred_element_type=F32)
                for i in range(LCH):
                    base = i * 2 * SEC
                    both = got[base:base + SEC] + got[base + SEC:base + 2 * SEC]
                    total = total + both * prof[j * LCH + i:j * LCH + i + 1]
            contrib[:, at] = total
            return c

        lax.fori_loop(0, PIX // TILE, gather, 0)
        owner = pix_ref[pl.ds(2, 1), :]
        slot = pix_ref[pl.ds(3, 1), :]
        want = (owner - owner // 2 * 2) * CY + slot
        slots = lax.broadcasted_iota(jnp.int32, (2 * CY, PIX), 0)
        hot = jnp.where(slots == want, 1.0, 0.0).astype(BF16)
        ch, cl = split(contrib[...])
        pair = owner // 2
        dims = (((1,), (1,)), ((), ()))

        def scatter(j, c):
            hs_, ls_ = [], []
            for i in range(8):
                mask = pair == j * 8 + i
                hs_.append(jnp.where(mask, ch, 0.0))
                ls_.append(jnp.where(mask, cl, 0.0))
            lh = jnp.concatenate(hs_, axis=0).astype(BF16)
            ll = jnp.concatenate(ls_, axis=0).astype(BF16)
            d = lax.dot_general(lh, hot, dims, preferred_element_type=F32)
            d = d + lax.dot_general(ll, hot, dims, preferred_element_type=F32)
            at = pl.ds(pl.multiple_of(j * 8 * SEC, 8 * SEC), 8 * SEC)
            dense_ref[0, at, :] = d[:, :CY]
            dense_ref[1, at, :] = d[:, CY:]
            return c

        lax.fori_loop(0, 8, scatter, 0)


def local(kap, adjoint, concentration, courant_x, courant_y, hx, hy, ker, kert, pix, wgt):
    def whole(a):
        return pl.BlockSpec(a.shape, lambda l, n=a.ndim: (0,) * n)

    field = pl.BlockSpec((SEC, 1, CX, CY), lambda l: (0, l, 0, 0))
    plane = pl.BlockSpec((1, CX, CY), lambda l: (l, 0, 0))
    return pl.pallas_call(
        local_kernel,
        grid=(LEV,),
        out_shape=(
            jax.ShapeDtypeStruct((SEC, LEV, CX, CY), F32),
            jax.ShapeDtypeStruct((2, 64 * SEC, CY), F32),
        ),
        in_specs=[
            whole(kap), field, field, plane, plane, whole(hx), whole(hy), whole(ker),
            whole(kert), whole(pix), whole(wgt),
        ],
        out_specs=(field, pl.BlockSpec((2, 64 * SEC, CY), lambda l: (0, 0, 0))),
        scratch_shapes=[
            pltpu.VMEM((LEV, 2 * SEC, CX * CY), BF16),
            pltpu.VMEM((SEC, PIX), F32),
        ],
        compiler_params=pltpu.CompilerParams(vmem_limit_bytes=56 << 20),
    )(kap, adjoint, concentration, courant_x, courant_y, hx, hy, ker, kert, pix, wgt)


def owners_kernel(d_ref, out_ref, d, rc, ra0, ra1, ra2, rb0, rb1, rb2, r20, r21, r22,
                  r30, r31, r32, ssem, rsem):
    x, y, z, c = place()

    def dev(axis, by):
        xx = lax.rem(x + by + 4, 4) if axis == 0 else x
        yy = lax.rem(y + by + 4, 4) if axis == 1 else y
        zz = lax.rem(z + by + 4, 4) if axis == 2 else z
        return (yy * 4 + xx, zz * 2 + c)

    sibling = (lax.axis_index("gx"), z * 2 + 1 - c)
    barrier = pltpu.get_barrier_semaphore()
    pl.semaphore_signal(barrier, 1, device_id=sibling, device_id_type=MESH)
    for axis in range(3):
        for by in (1, -1, 2):
            pl.semaphore_signal(barrier, 1, device_id=dev(axis, by), device_id_type=MESH)
    pl.semaphore_wait(barrier, 10)
    count = [0]

    def send(src, dst, peer):
        n = count[0]
        count[0] += 1
        copy = pltpu.make_async_remote_copy(
            src, dst, ssem.at[n], rsem.at[n], device_id=peer, device_id_type=MESH
        )
        copy.start()
        return copy

    mine = (x, y, z)

    def at(axis, by):
        return lax.rem(mine[axis] + by + 4, 4)

    def part(ref, band, fixed, lead=()):
        low, size = band
        idx = [slice(None)] * 3
        for axis, value in fixed.items():
            idx[(1, 0, 2)[axis]] = value
        return ref.at[tuple(lead) + tuple(idx) + (pl.ds(low, size),)]

    done = []
    first = send(d_ref.at[1 - c], rc, sibling)
    first.wait_recv()
    done.append(first)

    def total(i, carry):
        d[i // 4, lax.rem(i, 4)] = d_ref[c, i // 4, lax.rem(i, 4)] + rc[i // 4, lax.rem(i, 4)]
        return carry

    lax.fori_loop(0, 16, total, 0)
    ra, rb, r2, r3 = (ra0, ra1, ra2), (rb0, rb1, rb2), (r20, r21, r22), (r30, r31, r32)
    orders = ((0, 1, 2), (1, 2, 0), (2, 0, 1))
    step_a = []
    for g in range(3):
        a1 = orders[g][0]
        low, size = BANDS[g]
        half = size // 2 if size > 8 else 8
        ups = send(part(d, (low, half), {a1: at(a1, 2)}), ra[g].at[0], dev(a1, 1))
        downs = None
        if size > 8:
            downs = send(part(d, (low + half, half), {a1: at(a1, 2)}), ra[g].at[1], dev(a1, -1))
        step_a.append((ups, downs))
    step_b = []
    for g in range(3):
        a1 = orders[g][0]
        low, size = BANDS[g]
        half = size // 2 if size > 8 else 8
        ups, downs = step_a[g]
        ups.wait_recv()
        fwd = part(d, (low, half), {a1: at(a1, 1)})
        fwd[...] = fwd[...] + ra[g][0]
        if downs is not None:
            downs.wait_recv()
            fwd = part(d, (low + half, half), {a1: at(a1, -1)})
            fwd[...] = fwd[...] + ra[g][1]
        step_b.append((
            send(part(d, BANDS[g], {a1: at(a1, 1)}), rb[g].at[0], dev(a1, 1)),
            send(part(d, BANDS[g], {a1: at(a1, -1)}), rb[g].at[1], dev(a1, -1)),
        ))
        done.append(ups)
        if downs is not None:
            done.append(downs)
    step_2 = []
    for g in range(3):
        a1, a2, a3 = orders[g]
        for copy in step_b[g]:
            copy.wait_recv()
            done.append(copy)
        own = part(d, BANDS[g], {a1: mine[a1]})
        own[...] = own[...] + rb[g][0] + rb[g][1]
        step_2.append([
            send(part(d, BANDS[g], {a1: mine[a1], a2: at(a2, by)}), r2[g].at[i], dev(a2, by))
            for i, by in enumerate((1, -1, 2))
        ])
    step_3 = []
    for g in range(3):
        a1, a2, a3 = orders[g]
        for copy in step_2[g]:
            copy.wait_recv()
            done.append(copy)
        own = part(d, BANDS[g], {a1: mine[a1], a2: mine[a2]})
        own[...] = own[...] + r2[g][0] + r2[g][1] + r2[g][2]
        step_3.append([
            send(part(d, BANDS[g], {0: at(0, by if a3 == 0 else 0),
                                    1: at(1, by if a3 == 1 else 0),
                                    2: at(2, by if a3 == 2 else 0)}),
                 r3[g].at[i], dev(a3, by))
            for i, by in enumerate((1, -1, 2))
        ])
    for g in range(3):
        for copy in step_3[g]:
            copy.wait_recv()
            done.append(copy)
        low, size = BANDS[g]
        out_ref[pl.ds(low, size), :] = (
            d[y, x, z, pl.ds(low, size), :] + r3[g][0] + r3[g][1] + r3[g][2]
        )
    for copy in done:
        copy.wait_send()


def owners(dense):
    vmem = pl.BlockSpec(memory_space=pltpu.VMEM)

    def bands(*lead):
        return [pltpu.VMEM(tuple(lead) + (size, CY), F32) for _, size in BANDS]

    halves = [pltpu.VMEM((2, 4, 4, 8, CY), F32)] * 3
    return pl.pallas_call(
        owners_kernel,
        out_shape=jax.ShapeDtypeStruct((SEC, CY), F32),
        in_specs=[vmem],
        out_specs=vmem,
        scratch_shapes=[
            pltpu.VMEM((4, 4, 4, SEC, CY), F32),
            pltpu.VMEM((4, 4, 4, SEC, CY), F32),
            *halves,
            *bands(2, 4, 4),
            *bands(3, 4),
            *bands(3),
            pltpu.SemaphoreType.DMA((32,)),
            pltpu.SemaphoreType.DMA((32,)),
        ],
        compiler_params=pltpu.CompilerParams(
            collective_id=1, has_side_effects=True, vmem_limit_bytes=48 << 20
        ),
    )(dense)


def per_device(
    adjoint, concentration, courant_x, courant_y, diffusion, coag_kernel,
    pixel_column, pixel_owner, pixel_slot, pixel_level, pixel_weight,
):
    kap = jnp.broadcast_to(diffusion[:, None], (LEV, CY))
    pix = jnp.stack([pixel_column, pixel_level, pixel_owner[:, 0], pixel_slot])
    hx, hy = halos(kap, adjoint, courant_x, courant_y)
    out, dense = local(
        kap, adjoint, concentration, courant_x, courant_y, hx, hy, coag_kernel, coag_kernel.T,
        pix, pixel_weight[None, :],
    )
    return out, owners(dense.reshape(2, 4, 4, 4, SEC, CY))


def solution(mesh):
    pixels = P(("gx", "gy"))
    placed = (
        P(None, None, "gx", "gy"), P(None, None, "gx", "gy"), P(None, "gx", "gy"),
        P(None, "gx", "gy"), P(), P(), pixels, P(("gx", "gy"), None), pixels, pixels, pixels,
    )
    return jax.shard_map(
        per_device,
        mesh=mesh,
        in_specs=placed,
        out_specs=(P(None, None, "gx", "gy"), P(None, ("gx", "gy"))),
        check_vma=False,
    )
```

time: 815 us -> 82 us (0.10)
  waiting for transfers between devices: 664 us -> 0 us
  Pallas kernels: 0 us -> 69.9 us
  local copies, waits for them, and re-layouts: 66.1 us -> 9.36 us
  matrix products: 34 us -> 0 us
  other arithmetic: 28.4 us -> 1.38 us
  between operations: 14.3 us -> 0.67 us
    reduce_scatter x1 -> x0, waiting for transfers between devices: 655 us -> none  [per_device(): lax.psum_scatter(totals, ('gx', 'gy'), scatter_dimension=1, tiled=True)]
    pallas_call x0 -> x3, Pallas kernels: none -> 69.9 us  [the longest x1 30.7 us: local(): pl.pallas_call(local_kernel, grid=(LEV,), out_shape=(jax.ShapeDtypeStruct...]
    dot_general x3 -> x0, matrix products: 34 us -> none  [the longest x1 22.2 us: per_device(): jnp.einsum('klp,lp->kp', picked, profile, precision=lax.Precision.HIGHEST)]
    gather x1 -> x0, local copies, waits for them, and re-layouts: 22.2 us -> none  [per_device(): picked = jnp.take(columns, pixel_column, axis=2)]
    scatter-add x1 -> x0, other arithmetic: 16.9 us -> none  [per_device(): jnp.zeros((sections, peer_count * det_count), jnp.float32).at[:, target]]
    slice x5 -> x0, local copies, waits for them, and re-layouts: 11.9 us -> none  [the longest x2 7.59 us: extended(): leading = lax.slice_in_dim(shard, 0, width, axis=dim)]
    ppermute x4 -> x0, waiting for transfers between devices: 8.66 us -> none  [the longest x2 4.52 us: extended(): before = lax.ppermute(last, axis, up)]
  transfers between devices with their start and end apart: 5 -> 0, of which waited for: 3 -> 0; matrix products, arithmetic and copies ran while one was open for 2% -> 0% of each run, Pallas kernels for 0% -> 0%
where the time goes in v1:
time: 82 us; the launch traced here: 81.3 us
  Pallas kernels  69.9 us (85%)
  local copies, waits for them, and re-layouts  9.36 us (11%)
  other arithmetic  1.38 us (2%)
    pallas_call x1, Pallas kernels, local(): pl.pallas_call(local_kernel, grid=(LEV,), out_shape=(jax.ShapeDtypeStruct...  30.7 us
    pallas_call x1, Pallas kernels, owners(): pl.pallas_call(owners_kernel, out_shape=jax.ShapeDtypeStruct((SEC, CY), F...  23.9 us
    pallas_call x1, Pallas kernels, halos(): pl.pallas_call(halo_kernel, out_shape=(jax.ShapeDtypeStruct((2, SEC, LEV,...  15.3 us
    unnamed x16, local copies, waits for them, and re-layouts  8.63 us

profile of v1, /device:TPU:0, one launch (start us, length us, event | category | flops | bytes accessed | tf_op | source)
XLA Modules:
  0.0 81.3 jit_solution(3537455313285599386)
XLA Ops:
  0.6 0.7 broadcast_in_dim.4.kap_ref
  1.4 0.0 copy-start.5
  1.4 1.4 %copy.13 = f32[40,40]{0,1:T(8,128)} copy(f32[40,40]{1,0:T(8,128)} %ker_ref.1) | data formatting | bytes 12800 | tf_op args[5]
  2.8 1.4 %pad_add_fusion.pix_ref = s32[4,2048]{1,0:T(4,128)} fusion(s32[1,2048]{1,0:T(1,128)} %bitcast.10, s32[1,2048]{1,0:T(1,128)} %bitcast.11, s32[1,2048]{1,0:T(1,128)} %bitcast.12, s32[1,2048]{1,0:T(1,128)} %bitcast.13), kind=kLoop, calls=%fused_computation | loop fusion | flops 24576 | bytes 65536 | tf_op jit(solution)/shard_map/stack | solution.py:410
  4.2 0.0 copy-start
  4.2 1.7 %copy-done = f32[40,16,8,128]{3,2,1,0:T(8,128)S(1)} copy-done((f32[40,16,8,128]{3,2,1,0:T(8,128)S(1)}, f32[40,16,8,128]{3,2,1,0:T(8,128)}, u32[]{:S(2)}) %copy-start) | copy-done | bytes 2621464
  5.9 0.0 copy-start.3
  5.9 0.8 %copy-done.3 = f32[16,8,128]{2,1,0:T(8,128)S(1)} copy-done((f32[16,8,128]{2,1,0:T(8,128)S(1)}, f32[16,8,128]{2,1,0:T(8,128)}, u32[]{:S(2)}) %copy-start.3) | copy-done | bytes 65560
  6.7 0.0 copy-start.4
  6.7 0.8 %copy-done.4 = f32[16,8,128]{2,1,0:T(8,128)S(1)} copy-done((f32[16,8,128]{2,1,0:T(8,128)S(1)}, f32[16,8,128]{2,1,0:T(8,128)}, u32[]{:S(2)}) %copy-start.4) | copy-done | bytes 65560
  7.6 15.3 %shard_map.122 = (f32[2,40,16,128]{3,2,1,0:T(8,128)S(1)}, f32[2,40,128]{2,1,0:T(8,128)S(1)}) custom-call(f32[16,128]{1,0:T(8,128)S(1)} %broadcast_in_dim.4.kap_ref, f32[40,16,8,128]{3,2,1,0:T(8,128)S(1)} %copy-done, f32[16,8,128]{2,1,0:T(8,128)S(1)} %copy-done.3, f32[16,8,128]{2,1,0:T(8,128)S(1)} %copy-done.4), custom_call_target="tpu_custom_call" | custom-call | tf_op jit(solution)/shard_map/pallas_call | solution.py:104
  22.9 0.0 copy-start.2
  22.9 0.8 %copy-done.2 = f32[2,40,16,128]{3,2,1,0:T(8,128)} copy-done((f32[2,40,16,128]{3,2,1,0:T(8,128)}, f32[2,40,16,128]{3,2,1,0:T(8,128)S(1)}, u32[]{:S(2)}) %copy-start.2) | copy-done | bytes 655384
  23.7 0.0 copy-start.6
  23.7 0.6 copy-done.6
  24.4 0.0 copy-done.5
  24.4 30.7 %shard_map.123 = (f32[40,16,8,128]{3,2,1,0:T(8,128)}, f32[2,2560,128]{2,1,0:T(8,128)}) custom-call(f32[16,128]{1,0:T(8,128)} %copy-done.5, f32[40,16,8,128]{3,2,1,0:T(8,128)} %adj_ref.3, f32[40,16,8,128]{3,2,1,0:T(8,128)} %conc_ref.1, f32[16,8,128]{2,1,0:T(8,128)} %cx_ref.3, f32[16,8,128]{2,1,0:T(8,128)} %cy_ref.3, f32[2,40,16,128]{3,2,1,0:T(8,128)} %copy-done.2, ...), custom_call_target="tpu_custom_call" | custom-call | tf_op jit(solution)/shard_map/pallas_call | solution.py:236
  55.1 0.0 copy-start.1
  55.1 1.7 %copy-done.1 = f32[2,2560,128]{2,1,0:T(8,128)S(1)} copy-done((f32[2,2560,128]{2,1,0:T(8,128)S(1)}, f32[2,2560,128]{2,1,0:T(8,128)}, u32[]{:S(2)}) %copy-start.1) | copy-done | bytes 2621464
  56.8 23.9 %shard_map.124 = f32[40,128]{1,0:T(8,128)S(1)} custom-call(f32[2,4,4,4,40,128]{5,4,3,2,1,0:T(8,128)S(1)} %bitcast.7), custom_call_target="tpu_custom_call" | custom-call | tf_op jit(solution)/shard_map/pallas_call | solution.py:384
  80.7 0.6 copy.15
Async XLA Ops:
  1.4 23.0 %copy-start.5 = (f32[16,128]{1,0:T(8,128)}, f32[16,128]{1,0:T(8,128)S(1)}, u32[]{:S(2)}) copy-start(f32[16,128]{1,0:T(8,128)S(1)} %broadcast_in_dim.4.kap_ref) | copy-start | bytes 24580
  4.2 1.7 %copy-start = (f32[40,16,8,128]{3,2,1,0:T(8,128)S(1)}, f32[40,16,8,128]{3,2,1,0:T(8,128)}, u32[]{:S(2)}) copy-start(f32[40,16,8,128]{3,2,1,0:T(8,128)} %adj_ref.3) | copy-start | bytes 7864324
  5.9 0.8 %copy-start.3 = (f32[16,8,128]{2,1,0:T(8,128)S(1)}, f32[16,8,128]{2,1,0:T(8,128)}, u32[]{:S(2)}) copy-start(f32[16,8,128]{2,1,0:T(8,128)} %cx_ref.3) | copy-start | bytes 196612
  6.7 0.8 %copy-start.4 = (f32[16,8,128]{2,1,0:T(8,128)S(1)}, f32[16,8,128]{2,1,0:T(8,128)}, u32[]{:S(2)}) copy-start(f32[16,8,128]{2,1,0:T(8,128)} %cy_ref.3) | copy-start | bytes 196612
  22.9 0.8 %copy-start.2 = (f32[2,40,16,128]{3,2,1,0:T(8,128)}, f32[2,40,16,128]{3,2,1,0:T(8,128)S(1)}, u32[]{:S(2)}) copy-start(f32[2,40,16,128]{3,2,1,0:T(8,128)S(1)} %get-tuple-element.6.hx_ref) | copy-start | bytes 1966084
  23.7 0.6 copy-start.6
  55.1 1.7 %copy-start.1 = (f32[2,2560,128]{2,1,0:T(8,128)S(1)}, f32[2,2560,128]{2,1,0:T(8,128)}, u32[]{:S(2)}) copy-start(f32[2,2560,128]{2,1,0:T(8,128)} %get-tuple-element.9) | copy-start | bytes 7864324

commit v2 on v0

v2 whole, which is shorter than its diff:
```python
import jax
import jax.numpy as jnp
from jax import lax
from jax.experimental import pallas as pl
from jax.experimental.pallas import tpu as pltpu
from jax.sharding import PartitionSpec as P

MESH = pl.DeviceIdType.MESH
F32 = jnp.float32
BF16 = jnp.bfloat16
SEC, LEV, CX, CY = 40, 16, 8, 128
PIX = 2048
LCH = 4
TILE = 256
BANDS = ((0, 16), (16, 16), (32, 8))


def split(v):
    hi = v.astype(BF16).astype(F32)
    return hi, v - hi


def place():
    gx = lax.axis_index("gx")
    gy = lax.axis_index("gy")
    return lax.rem(gx, 4), gx // 4, gy // 2, lax.rem(gy, 2)


EAST, WEST, NORTH, SOUTH, KEEP = range(5)
ORDERS = ((0, 1, 2), (1, 2, 0), (2, 0, 1))


def kernel(
    adj_h, conc_h, cx_h, cy_h, dif_ref, ker_h, col_h, own_h, slot_h, lev_h, wgt_h,
    out_ref, grad_ref,
    adj, conc, cx, cy, ker, col, own, slot, lev, wgt,
    coef, k3, k3t, px, py, rx, ry, cells, hot, prof, pairs, held0, held1, held2, contrib,
    d0, d1, d2, rc0, rc1, rc2, ra0, ra1, ra2, rb0, rb1, rb2, r20, r21, r22, r30, r31, r32,
    lsem, ssem, rsem,
):
    gx = lax.axis_index("gx")
    gy = lax.axis_index("gy")
    x, y, z, c = place()
    mine = (x, y, z)
    half_peers = (
        (lax.rem(gx + 15, 16), gy),
        (lax.rem(gx + 1, 16), gy),
        (gx, lax.rem(gy + 7, 8)),
        (gx, lax.rem(gy + 1, 8)),
    )

    def at(axis, by):
        return lax.rem(mine[axis] + by + 4, 4)

    def dev(axis, by):
        xx = at(0, by) if axis == 0 else x
        yy = at(1, by) if axis == 1 else y
        zz = at(2, by) if axis == 2 else z
        return (yy * 4 + xx, zz * 2 + c)

    sibling = (gx, z * 2 + 1 - c)
    barrier = pltpu.get_barrier_semaphore()
    for peer in half_peers:
        pl.semaphore_signal(barrier, 1, device_id=peer, device_id_type=MESH)
    pl.semaphore_signal(barrier, 1, device_id=sibling, device_id_type=MESH)
    for axis in range(3):
        for by in (1, -1, 2):
            pl.semaphore_signal(barrier, 1, device_id=dev(axis, by), device_id_type=MESH)
    loads = {}
    for i, (name, src, dst) in enumerate((
        ("cx", cx_h, cx), ("cy", cy_h, cy), ("adj", adj_h, adj), ("conc", conc_h, conc),
        ("ker", ker_h, ker), ("col", col_h, col), ("own", own_h, own), ("slot", slot_h, slot),
        ("lev", lev_h, lev), ("wgt", wgt_h, wgt),
    )):
        loads[name] = pltpu.make_async_copy(src, dst, lsem.at[i])
        loads[name].start()
    count = [0]
    done = []

    def send(src, dst, peer):
        n = count[0]
        count[0] += 1
        copy = pltpu.make_async_remote_copy(
            src, dst, ssem.at[n], rsem.at[n], device_id=peer, device_id_type=MESH
        )
        copy.start()
        done.append(copy)
        return copy

    loads["cx"].wait()
    loads["cy"].wait()

    def factors(l, carry):
        kap = dif_ref[l]
        a, b = cx[l], cy[l]
        coef[EAST, l] = jnp.maximum(a, 0.0) + kap
        coef[WEST, l] = jnp.maximum(-a, 0.0) + kap
        coef[NORTH, l] = jnp.maximum(b, 0.0) + kap
        coef[SOUTH, l] = jnp.maximum(-b, 0.0) + kap
        coef[KEEP, l] = 1.0 - jnp.abs(a) - jnp.abs(b) - 4.0 * kap
        return carry

    lax.fori_loop(0, LEV, factors, 0)
    loads["adj"].wait()
    first = coef[EAST, :, 0, :]
    last = coef[WEST, :, CX - 1, :]

    def fill(k, carry):
        px[0, k] = adj[k, :, 0, :] * first
        px[1, k] = adj[k, :, CX - 1, :] * last
        return carry

    lax.fori_loop(0, SEC, fill, 0)
    pl.semaphore_wait(barrier, 14)
    sent_x = [send(px.at[i], rx.at[i], half_peers[i]) for i in range(2)]
    lane = lax.broadcasted_iota(jnp.int32, (SEC, CY), 1)
    row = lax.broadcasted_iota(jnp.int32, (SEC, CY), 0)

    def edge(l, carry):
        low, high = carry
        for i in range(CX):
            a = adj[:, l, i, :]
            q = l * CX + i
            s = pltpu.roll(a * coef[NORTH, l, pl.ds(i, 1), :], q, 1)
            n = pltpu.roll(a * coef[SOUTH, l, pl.ds(i, 1), :], q + 1, 1)
            low = jnp.where(lane == q, s, low)
            high = jnp.where(lane == q, n, high)
        return low, high

    zero = jnp.zeros((SEC, CY), F32)
    low, high = lax.fori_loop(0, LEV, edge, (zero, zero))
    py[0] = low
    py[1] = high
    sent_y = [send(py.at[i], ry.at[i], half_peers[2 + i]) for i in range(2)]

    for name in ("ker", "col", "own", "slot", "lev", "wgt", "conc"):
        loads[name].wait()
    kh, kl = split(ker[...])
    k3[...] = jnp.concatenate([kh, kh, kl], axis=1).astype(BF16)
    kh, kl = split(ker[...].T)
    k3t[...] = jnp.concatenate([kh, kh, kl], axis=1).astype(BF16)
    height = lax.broadcasted_iota(jnp.int32, (LEV, PIX), 0).astype(F32) - lev[...].astype(F32)
    shape = jnp.exp(-height * height / 8.0)
    prof[...] = shape / jnp.sum(shape, axis=0, keepdims=True) * wgt[...]
    pair = own[...] // 2
    pairs[...] = jnp.broadcast_to(pair.astype(F32), (16, PIX)).astype(BF16)
    want = (own[...] - pair * 2) * CY + slot[...]

    def mark(i, carry):
        base = pl.multiple_of(i * 64, 64)
        ids = lax.broadcasted_iota(jnp.int32, (64, PIX), 0) + base
        cells[pl.ds(base, 64), :] = jnp.where(ids == col[...], 1.0, 0.0).astype(BF16)
        return carry

    lax.fori_loop(0, CX * CY // 64, mark, 0)
    for i in range(4):
        ids = lax.broadcasted_iota(jnp.int32, (64, PIX), 0) + i * 64
        hot[pl.ds(i * 64, 64), :] = jnp.where(ids == want, 1.0, 0.0).astype(BF16)

    def product(k, v):
        vh, vl = split(v)
        v3 = jnp.concatenate([vh, vl, vh], axis=0).astype(BF16)
        return jnp.dot(k[...], v3, preferred_element_type=F32)

    helds = (held0, held1, held2)
    far_e = jnp.where(gx == 15, 0.0, 1.0)
    far_w = jnp.where(gx == 0, 0.0, 1.0)
    far_n = jnp.where(gy == 7, 0.0, 1.0)
    far_s = jnp.where(gy == 0, 0.0, 1.0)

    def level(xs):
        def step(l, carry):
            turn = lax.rem(CY - l * CX, CY)
            hn = pltpu.roll(ry[0], turn, 1) * far_n
            hs = pltpu.roll(ry[1], turn, 1) * far_s

            def cf(kind, i):
                return coef[kind, l, pl.ds(i, 1), :]

            moved, ups, concs = [], [], []
            for i in xs:
                a = adj[:, l, i, :]
                m = cf(KEEP, i) * a
                if i < CX - 1:
                    m = m + cf(EAST, i + 1) * adj[:, l, i + 1, :]
                else:
                    m = m + rx[0, :, l, :] * far_e
                if i > 0:
                    m = m + cf(WEST, i - 1) * adj[:, l, i - 1, :]
                else:
                    m = m + rx[1, :, l, :] * far_w
                nh = pltpu.roll(hn, (CY - i) % CY, 1)
                sh = pltpu.roll(hs, (CY - 1 - i) % CY, 1)
                m = m + pltpu.roll(jnp.where(lane == 0, nh, cf(NORTH, i) * a), CY - 1, 1)
                m = m + pltpu.roll(jnp.where(lane == CY - 1, sh, cf(SOUTH, i) * a), 1, 1)
                nxt = jnp.where(row == SEC - 1, 0.0, pltpu.roll(m, SEC - 1, 0))
                moved.append(m)
                ups.append(nxt - m)
                concs.append(conc[:, l, i, :])
            m = jnp.concatenate(moved, axis=1)
            up = jnp.concatenate(ups, axis=1)
            cc = jnp.concatenate(concs, axis=1)
            res = m + up * product(k3, cc) + product(k3t, up * cc)
            rh, rl = split(res)
            for n, i in enumerate(xs):
                out_ref[:, l, i, :] = res[:, n * CY:(n + 1) * CY]
            for b, (start, size) in enumerate(BANDS):
                both = jnp.concatenate([rh[start:start + size], rl[start:start + size]], axis=0)
                both = both.astype(BF16)
                for n, i in enumerate(xs):
                    helds[b][l, :, i * CY:(i + 1) * CY] = both[:, n * CY:(n + 1) * CY]
            return carry

        lax.fori_loop(0, LEV, step, 0)

    for copy in sent_y:
        copy.wait_recv()
    level(range(1, CX - 1))
    for copy in sent_x:
        copy.wait_recv()
    level((0, CX - 1))

    ds, rc = (d0, d1, d2), (rc0, rc1, rc2)
    ra, rb, r2, r3 = (ra0, ra1, ra2), (rb0, rb1, rb2), (r20, r21, r22), (r30, r31, r32)

    def gather(b):
        size = BANDS[b][1]
        group = 256 // (2 * size)

        def tile(t, carry):
            where = pl.ds(pl.multiple_of(t * TILE, TILE), TILE)
            total = jnp.zeros((size, TILE), F32)
            for j in range(LEV // group):
                block = helds[b][pl.ds(j * group, group)].reshape(256, CX * CY)
                got = jnp.dot(block, cells[:, where], preferred_element_type=F32)
                for i in range(group):
                    base = i * 2 * size
                    both = got[base:base + size] + got[base + size:base + 2 * size]
                    total = total + both * prof[pl.ds(j * group + i, 1), where]
            contrib[pl.ds(0, size), where] = total
            return carry

        lax.fori_loop(0, PIX // TILE, tile, 0)

    dims = (((1,), (1,)), ((), ()))

    def scatter(b):
        size = BANDS[b][1]
        ch, cl = split(contrib[pl.ds(0, size), :])
        if size == 8:
            ch = jnp.concatenate([ch, cl], axis=0)
        ch = ch.astype(BF16)
        cl = cl.astype(BF16)
        none = jnp.zeros((16, PIX), BF16)
        copies = []
        for j in range(4):
            def rows(v):
                return jnp.concatenate(
                    [jnp.where(pairs[...] == float(j * 16 + i), v, none) for i in range(16)], axis=0
                )

            got = lax.dot_general(rows(ch), hot[...], dims, preferred_element_type=F32)
            if size == 16:
                got = got + lax.dot_general(rows(cl), hot[...], dims, preferred_element_type=F32)
                got = got.reshape(4, 4, 16, 2 * CY)
            else:
                got = got.reshape(4, 4, 16, 2 * CY)
                got = got[:, :, :8] + got[:, :, 8:]
            ds[b][0, j] = got[..., :CY]
            ds[b][1, j] = got[..., CY:]
            copies.append(send(ds[b].at[1 - c, j], rc[b].at[j], sibling))
        return copies

    def part(b, fixed, low, size):
        idx = [slice(None)] * 3
        for axis, value in fixed.items():
            idx[(1, 0, 2)[axis]] = value
        return ds[b].at[(c,) + tuple(idx) + (pl.ds(low, size),)]

    def stage_c(b, copies):
        for copy in copies:
            copy.wait_recv()

        def add(i, carry):
            j, k = i // 4, lax.rem(i, 4)
            ds[b][c, j, k] = ds[b][c, j, k] + rc[b][j, k]
            return carry

        lax.fori_loop(0, 16, add, 0)
        a1 = ORDERS[b][0]
        size = BANDS[b][1]
        out = [send(part(b, {a1: at(a1, 2)}, 0, 8), ra[b].at[0], dev(a1, 1))]
        if size > 8:
            out.append(send(part(b, {a1: at(a1, 2)}, 8, 8), ra[b].at[1], dev(a1, -1)))
        return out

    def stage_a(b, copies):
        a1 = ORDERS[b][0]
        for n, copy in enumerate(copies):
            copy.wait_recv()
            fwd = part(b, {a1: at(a1, (1, -1)[n])}, 8 * n, 8)
            fwd[...] = fwd[...] + ra[b][n]
        size = BANDS[b][1]
        return [
            send(part(b, {a1: at(a1, by)}, 0, size), rb[b].at[i], dev(a1, by))
            for i, by in enumerate((1, -1))
        ]

    def stage_b(b, copies):
        a1, a2, a3 = ORDERS[b]
        size = BANDS[b][1]
        for copy in copies:
            copy.wait_recv()
        here = part(b, {a1: mine[a1]}, 0, size)
        here[...] = here[...] + rb[b][0] + rb[b][1]
        return [
            send(part(b, {a1: mine[a1], a2: at(a2, by)}, 0, size), r2[b].at[i], dev(a2, by))
            for i, by in enumerate((1, -1, 2))
        ]

    def stage_2(b, copies):
        a1, a2, a3 = ORDERS[b]
        size = BANDS[b][1]
        for copy in copies:
            copy.wait_recv()
        here = part(b, {a1: mine[a1], a2: mine[a2]}, 0, size)
        here[...] = here[...] + r2[b][0] + r2[b][1] + r2[b][2]
        return [
            send(part(b, {n: at(n, by if n == a3 else 0) for n in range(3)}, 0, size),
                 r3[b].at[i], dev(a3, by))
            for i, by in enumerate((1, -1, 2))
        ]

    def stage_3(b, copies):
        start, size = BANDS[b]
        for copy in copies:
            copy.wait_recv()
        grad_ref[pl.ds(start, size), :] = ds[b][c, y, x, z] + r3[b][0] + r3[b][1] + r3[b][2]

    gather(0)
    a = scatter(0)
    gather(1)
    a = stage_c(0, a)
    b = scatter(1)
    a = stage_a(0, a)
    gather(2)
    b = stage_c(1, b)
    e = scatter(2)
    a = stage_b(0, a)
    b = stage_a(1, b)
    e = stage_c(2, e)
    a = stage_2(0, a)
    e = stage_a(2, e)
    b = stage_b(1, b)
    stage_3(0, a)
    e = stage_b(2, e)
    b = stage_2(1, b)
    e = stage_2(2, e)
    stage_3(1, b)
    stage_3(2, e)
    for copy in done:
        copy.wait_send()


def per_device(
    adjoint, concentration, courant_x, courant_y, diffusion, coag_kernel,
    pixel_column, pixel_owner, pixel_slot, pixel_level, pixel_weight,
):
    vmem = pl.BlockSpec(memory_space=pltpu.VMEM)
    smem = pl.BlockSpec(memory_space=pltpu.SMEM)
    hbm = pl.BlockSpec(memory_space=pltpu.HBM)
    field = (SEC, LEV, CX, CY)
    plane = (LEV, CX, CY)

    def bands(*lead):
        return [pltpu.VMEM(tuple(lead) + (size, CY), F32) for _, size in BANDS]

    ints = pltpu.VMEM((1, PIX), jnp.int32)
    return pl.pallas_call(
        kernel,
        out_shape=(
            jax.ShapeDtypeStruct(field, F32),
            jax.ShapeDtypeStruct((SEC, CY), F32),
        ),
        in_specs=[hbm, hbm, hbm, hbm, smem] + [hbm] * 6,
        out_specs=(vmem, vmem),
        scratch_shapes=[
            pltpu.VMEM(field, F32), pltpu.VMEM(field, F32),
            pltpu.VMEM(plane, F32), pltpu.VMEM(plane, F32),
            pltpu.VMEM((SEC, SEC), F32),
            ints, ints, ints, ints, pltpu.VMEM((1, PIX), F32),
            pltpu.VMEM((5,) + plane, F32),
            pltpu.VMEM((SEC, 3 * SEC), BF16), pltpu.VMEM((SEC, 3 * SEC), BF16),
            pltpu.VMEM((2, SEC, LEV, CY), F32), pltpu.VMEM((2, SEC, CY), F32),
            pltpu.VMEM((2, SEC, LEV, CY), F32), pltpu.VMEM((2, SEC, CY), F32),
            pltpu.VMEM((CX * CY, PIX), BF16), pltpu.VMEM((2 * CY, PIX), BF16),
            pltpu.VMEM((LEV, PIX), F32), pltpu.VMEM((16, PIX), BF16),
            *[pltpu.VMEM((LEV, 2 * size, CX * CY), BF16) for _, size in BANDS],
            pltpu.VMEM((16, PIX), F32),
            *bands(2, 4, 4, 4),
            *bands(4, 4, 4),
            *[pltpu.VMEM((size // 8, 4, 4, 8, CY), F32) for _, size in BANDS],
            *bands(2, 4, 4),
            *bands(3, 4),
            *bands(3),
            pltpu.SemaphoreType.DMA((10,)),
            pltpu.SemaphoreType.DMA((48,)),
            pltpu.SemaphoreType.DMA((48,)),
        ],
        compiler_params=pltpu.CompilerParams(
            collective_id=0, has_side_effects=True, vmem_limit_bytes=56 << 20
        ),
    )(
        adjoint, concentration, courant_x, courant_y, diffusion, coag_kernel,
        pixel_column[None, :], pixel_owner[:, 0][None, :], pixel_slot[None, :],
        pixel_level[None, :], pixel_weight[None, :],
    )


def solution(mesh):
    pixels = P(("gx", "gy"))
    placed = (
        P(None, None, "gx", "gy"), P(None, None, "gx", "gy"), P(None, "gx", "gy"),
        P(None, "gx", "gy"), P(), P(), pixels, P(("gx", "gy"), None), pixels, pixels, pixels,
    )
    return jax.shard_map(
        per_device,
        mesh=mesh,
        in_specs=placed,
        out_specs=(P(None, None, "gx", "gy"), P(None, ("gx", "gy"))),
        check_vma=False,
    )
```

time: 815 us -> 76 us (0.09)
  waiting for transfers between devices: 664 us -> 0 us
  Pallas kernels: 0 us -> 71 us
  local copies, waits for them, and re-layouts: 66.1 us -> 4.15 us
  matrix products: 34 us -> 0 us
  other arithmetic: 28.4 us -> 0 us
  between operations: 14.3 us -> 0.65 us
    reduce_scatter x1 -> x0, waiting for transfers between devices: 655 us -> none  [per_device(): lax.psum_scatter(totals, ('gx', 'gy'), scatter_dimension=1, tiled=True)]
    pallas_call x0 -> x1, Pallas kernels: none -> 71 us  [per_device(): pl.pallas_call(kernel, out_shape=(jax.ShapeDtypeStruct(field, F32), jax.S...]
    dot_general x3 -> x0, matrix products: 34 us -> none  [the longest x1 22.2 us: per_device(): jnp.einsum('klp,lp->kp', picked, profile, precision=lax.Precision.HIGHEST)]
    gather x1 -> x0, local copies, waits for them, and re-layouts: 22.2 us -> none  [per_device(): picked = jnp.take(columns, pixel_column, axis=2)]
    scatter-add x1 -> x0, other arithmetic: 16.9 us -> none  [per_device(): jnp.zeros((sections, peer_count * det_count), jnp.float32).at[:, target]]
    slice x5 -> x0, local copies, waits for them, and re-layouts: 11.9 us -> none  [the longest x2 7.59 us: extended(): leading = lax.slice_in_dim(shard, 0, width, axis=dim)]
    ppermute x4 -> x0, waiting for transfers between devices: 8.66 us -> none  [the longest x2 4.52 us: extended(): before = lax.ppermute(last, axis, up)]
    unnamed x34 -> x4, local copies, waits for them, and re-layouts: 12.4 us -> 4.15 us
  transfers between devices with their start and end apart: 5 -> 0, of which waited for: 3 -> 0; matrix products, arithmetic and copies ran while one was open for 2% -> 0% of each run, Pallas kernels for 0% -> 0%
where the time goes in v2:
time: 76 us; the launch traced here: 75.8 us
  Pallas kernels  71 us (93%)
  local copies, waits for them, and re-layouts  4.15 us (5%)
    pallas_call x1, Pallas kernels, per_device(): pl.pallas_call(kernel, out_shape=(jax.ShapeDtypeStruct(field, F32), jax.S...  71 us
    unnamed x4, local copies, waits for them, and re-layouts  4.15 us

profile of v2, /device:TPU:0, one launch (start us, length us, event | category | flops | bytes accessed | tf_op | source)
XLA Modules:
  0.0 75.8 jit_solution(7952429153721752701)
XLA Ops:
  0.6 71.0 %shard_map.122 = (f32[40,16,8,128]{3,2,1,0:T(8,128)}, f32[40,128]{1,0:T(8,128)}) custom-call(f32[40,16,8,128]{3,2,1,0:T(8,128)} %adj_h.1, f32[40,16,8,128]{3,2,1,0:T(8,128)} %conc_h.1, f32[16,8,128]{2,1,0:T(8,128)} %cx_h.1, f32[16,8,128]{2,1,0:T(8,128)} %cy_h.1, f32[16]{0:T(128)} %dif_ref.1, f32[40,40]{1,0:T(8,128)} %ker_h.1, s32[1,2048]{1,0:T(1,128)} %bitcast.5, ...), custom_call_target="tpu_custom_call" | custom-call | tf_op jit(solution)/shard_map/pallas_call | solution.py:379
  71.6 0.0 copy-start
  71.7 3.5 %copy.15 = f32[40,16,8,128]{3,2,1,0:T(8,128)} copy(f32[40,16,8,128]{3,2,1,0:T(8,128)} %get-tuple-element.4) | data formatting | bytes 5242880
  75.2 0.0 copy-done
  75.2 0.6 copy.16
Async XLA Ops:
  71.6 3.6 %copy-start = (f32[40,128]{1,0:T(8,128)S(1)}, f32[40,128]{1,0:T(8,128)}, u32[]{:S(2)}) copy-start(f32[40,128]{1,0:T(8,128)} %get-tuple-element.5) | copy-start | bytes 61444

commit v3 on v2

v3 whole, which is shorter than its diff:
```python
import jax
import jax.numpy as jnp
from jax import lax
from jax.experimental import pallas as pl
from jax.experimental.pallas import tpu as pltpu
from jax.sharding import PartitionSpec as P

MESH = pl.DeviceIdType.MESH
F32 = jnp.float32
BF16 = jnp.bfloat16
SEC, LEV, CX, CY = 40, 16, 8, 128
PIX = 2048
TILE = 1024
LCH = 4
BANDS = tuple((8 * b, 8) for b in range(5))
ORDERS = ((0, 1, 2), (1, 2, 0), (2, 0, 1), (0, 1, 2), (1, 2, 0))
GROUP_IN = 2
GROUP_OUT = 4
PLAN = (
    (0, 0), (1, 0), (0, 1), (2, 0), (1, 1), (3, 0), (2, 1), (4, 0),
    (0, 2), (3, 1), (4, 1), (1, 2), (0, 3), (2, 2), (1, 3), (3, 2), (2, 3), (0, 4), (4, 2),
    (1, 4), (3, 3), (2, 4), (4, 3), (3, 4), (4, 4),
)


def split(v):
    hi = v.astype(BF16).astype(F32)
    return hi, v - hi


def place():
    gx = lax.axis_index("gx")
    gy = lax.axis_index("gy")
    return lax.rem(gx, 4), gx // 4, gy // 2, lax.rem(gy, 2)


EAST, WEST, NORTH, SOUTH, KEEP = range(5)


def kernel(
    adj_h, conc_h, cx_h, cy_h, dif_ref, ker_h, col_h, own_h, slot_h, lev_h, wgt_h,
    out_ref, grad_ref,
    adj, conc, cx, cy, ker, col, own, slot, lev, wgt,
    coef, k3, k3t, px, py, rx, ry, cells, hot, prof, pairs, held, contrib, res,
    ds, rc, r1, r2, r3, lsem, osem, ssem, rsem,
):
    gx = lax.axis_index("gx")
    gy = lax.axis_index("gy")
    x, y, z, c = place()
    mine = (x, y, z)
    half_peers = (
        (lax.rem(gx + 15, 16), gy),
        (lax.rem(gx + 1, 16), gy),
        (gx, lax.rem(gy + 7, 8)),
        (gx, lax.rem(gy + 1, 8)),
    )

    def at(axis, by):
        return lax.rem(mine[axis] + by + 4, 4)

    def dev(axis, by):
        xx = at(0, by) if axis == 0 else x
        yy = at(1, by) if axis == 1 else y
        zz = at(2, by) if axis == 2 else z
        return (yy * 4 + xx, zz * 2 + c)

    sibling = (gx, z * 2 + 1 - c)
    barrier = pltpu.get_barrier_semaphore()
    for peer in half_peers:
        pl.semaphore_signal(barrier, 1, device_id=peer, device_id_type=MESH)
    pl.semaphore_signal(barrier, 1, device_id=sibling, device_id_type=MESH)
    for axis in range(3):
        for by in (1, -1, 2):
            pl.semaphore_signal(barrier, 1, device_id=dev(axis, by), device_id_type=MESH)
    loads = {}
    for i, (name, src, dst) in enumerate((
        ("cx", cx_h, cx), ("cy", cy_h, cy), ("adj", adj_h, adj), ("conc", conc_h, conc),
        ("ker", ker_h, ker), ("col", col_h, col), ("own", own_h, own), ("slot", slot_h, slot),
        ("lev", lev_h, lev), ("wgt", wgt_h, wgt),
    )):
        loads[name] = pltpu.make_async_copy(src, dst, lsem.at[i])
        loads[name].start()
    count = [0]
    done = []

    def send(src, dst, peer):
        n = count[0]
        count[0] += 1
        copy = pltpu.make_async_remote_copy(
            src, dst, ssem.at[n], rsem.at[n], device_id=peer, device_id_type=MESH
        )
        copy.start()
        done.append(copy)
        return copy

    loads["cx"].wait()
    loads["cy"].wait()

    def factors(l, carry):
        kap = dif_ref[l]
        a, b = cx[l], cy[l]
        coef[EAST, l] = jnp.maximum(a, 0.0) + kap
        coef[WEST, l] = jnp.maximum(-a, 0.0) + kap
        coef[NORTH, l] = jnp.maximum(b, 0.0) + kap
        coef[SOUTH, l] = jnp.maximum(-b, 0.0) + kap
        coef[KEEP, l] = 1.0 - jnp.abs(a) - jnp.abs(b) - 4.0 * kap
        return carry

    lax.fori_loop(0, LEV, factors, 0)
    loads["adj"].wait()
    first = coef[EAST, :, 0, :]
    last = coef[WEST, :, CX - 1, :]

    def fill(part):
        rows = slice(8 * part, 8 * part + 8)

        def one(k, carry):
            px[0, part, k] = adj[k, rows, 0, :] * first[rows]
            px[1, part, k] = adj[k, rows, CX - 1, :] * last[rows]
            return carry

        lax.fori_loop(0, SEC, one, 0, unroll=4)

    fill(0)
    pl.semaphore_wait(barrier, 14)
    sent_x = [[send(px.at[i, 0], rx.at[i, 0], half_peers[i]) for i in range(2)]]
    fill(1)
    sent_x.append([send(px.at[i, 1], rx.at[i, 1], half_peers[i]) for i in range(2)])
    lane = lax.broadcasted_iota(jnp.int32, (SEC, CY), 1)
    row = lax.broadcasted_iota(jnp.int32, (SEC, CY), 0)

    def edge(l, carry):
        low, high = carry
        for i in range(CX):
            a = adj[:, l, i, :]
            q = l * CX + i
            s = pltpu.roll(a * coef[NORTH, l, pl.ds(i, 1), :], q, 1)
            n = pltpu.roll(a * coef[SOUTH, l, pl.ds(i, 1), :], q + 1, 1)
            low = jnp.where(lane == q, s, low)
            high = jnp.where(lane == q, n, high)
        return low, high

    zero = jnp.zeros((SEC, CY), F32)
    low, high = lax.fori_loop(0, LEV, edge, (zero, zero))
    py[0] = low
    py[1] = high
    sent_y = [send(py.at[i], ry.at[i], half_peers[2 + i]) for i in range(2)]

    for name in ("ker", "col", "own", "slot", "lev", "wgt", "conc"):
        loads[name].wait()
    kh, kl = split(ker[...])
    k3[...] = jnp.concatenate([kh, kh, kl], axis=1).astype(BF16)
    kh, kl = split(ker[...].T)
    k3t[...] = jnp.concatenate([kh, kh, kl], axis=1).astype(BF16)
    height = lax.broadcasted_iota(jnp.int32, (LEV, PIX), 0).astype(F32) - lev[...].astype(F32)
    shape = jnp.exp(-height * height / 8.0)
    prof[...] = shape / jnp.sum(shape, axis=0, keepdims=True) * wgt[...]
    pair = own[...] // 2
    pairs[...] = jnp.broadcast_to(pair.astype(F32), (16, PIX)).astype(BF16)
    want = (own[...] - pair * 2) * CY + slot[...]

    turned = lax.rem(col[...] + (CX - 1) * CY, CX * CY)

    def mark(i, carry):
        base = pl.multiple_of(i * 64, 64)
        ids = lax.broadcasted_iota(jnp.int32, (64, PIX), 0) + base
        cells[pl.ds(base, 64), :] = jnp.where(ids == turned, 1.0, 0.0).astype(BF16)
        return carry

    lax.fori_loop(0, CX * CY // 64, mark, 0)
    for i in range(4):
        ids = lax.broadcasted_iota(jnp.int32, (64, PIX), 0) + i * 64
        hot[pl.ds(i * 64, 64), :] = jnp.where(ids == want, 1.0, 0.0).astype(BF16)

    def product(k, v):
        vh, vl = split(v)
        v3 = jnp.concatenate([vh, vl, vh], axis=0).astype(BF16)
        return jnp.dot(k[...], v3, preferred_element_type=F32)

    far_e = jnp.where(gx == 15, 0.0, 1.0)
    far_w = jnp.where(gx == 0, 0.0, 1.0)
    far_n = jnp.where(gy == 7, 0.0, 1.0)
    far_s = jnp.where(gy == 0, 0.0, 1.0)

    def levels(xs, group, start, stop):
        def step(it, carry):
            moved, ups, concs = [], [], []
            for g in range(group):
                l = it * group + g
                turn = lax.rem(CY - l * CX, CY)
                hn = pltpu.roll(ry[0], turn, 1) * far_n
                hs = pltpu.roll(ry[1], turn, 1) * far_s

                def cf(kind, i):
                    return coef[kind, l, pl.ds(i, 1), :]

                for i in xs:
                    a = adj[:, l, i, :]
                    m = cf(KEEP, i) * a
                    if i < CX - 1:
                        m = m + cf(EAST, i + 1) * adj[:, l, i + 1, :]
                    else:
                        m = m + rx[0, l // 8, :, lax.rem(l, 8), :] * far_e
                    if i > 0:
                        m = m + cf(WEST, i - 1) * adj[:, l, i - 1, :]
                    else:
                        m = m + rx[1, l // 8, :, lax.rem(l, 8), :] * far_w
                    nh = pltpu.roll(hn, (CY - i) % CY, 1)
                    sh = pltpu.roll(hs, (CY - 1 - i) % CY, 1)
                    m = m + pltpu.roll(jnp.where(lane == 0, nh, cf(NORTH, i) * a), CY - 1, 1)
                    m = m + pltpu.roll(jnp.where(lane == CY - 1, sh, cf(SOUTH, i) * a), 1, 1)
                    nxt = jnp.where(row == SEC - 1, 0.0, pltpu.roll(m, SEC - 1, 0))
                    moved.append(m)
                    ups.append(nxt - m)
                    concs.append(conc[:, l, i, :])
            m = jnp.concatenate(moved, axis=1)
            up = jnp.concatenate(ups, axis=1)
            cc = jnp.concatenate(concs, axis=1)
            new = m + up * product(k3, cc) + product(k3t, up * cc)
            rh, rl = split(new)
            both = jnp.concatenate([rh, rl], axis=0).astype(BF16)
            n = 0
            for g in range(group):
                l = it * group + g
                at_row = pl.ds(pl.multiple_of(l * 2 * SEC, 2 * SEC), 2 * SEC)
                for i in xs:
                    lanes = slice(n * CY, (n + 1) * CY)
                    spot = (i + CX - 1) % CX * CY
                    res[:, l, i, :] = new[:, lanes]
                    held[at_row, spot:spot + CY] = both[:, lanes]
                    n += 1
            return carry

        lax.fori_loop(start, stop, step, 0)

    def gather(low, high, more):
        def tile(t, carry):
            where = pl.ds(pl.multiple_of(t * TILE, TILE), TILE)
            total = contrib[:, where] if more else jnp.zeros((SEC, TILE), F32)
            onehot = cells[low:high, where]
            for j in range(0, LEV, LCH):
                block = held[j * 2 * SEC:(j + LCH) * 2 * SEC, low:high]
                got = jnp.dot(block, onehot, preferred_element_type=F32)
                for l in range(LCH):
                    base = l * 2 * SEC
                    both = got[base:base + SEC] + got[base + SEC:base + 2 * SEC]
                    total = total + both * prof[pl.ds(j + l, 1), where]
            contrib[:, where] = total
            return carry

        lax.fori_loop(0, PIX // TILE, tile, 0)

    for copy in sent_y:
        copy.wait_recv()
    levels(range(1, CX - 1), GROUP_IN, 0, LEV // GROUP_IN)
    gather(0, 6 * CY, False)
    for n in range(2):
        for copy in sent_x[n]:
            copy.wait_recv()
        levels((CX - 1, 0), GROUP_OUT, n * 8 // GROUP_OUT, (n + 1) * 8 // GROUP_OUT)
    out = pltpu.make_async_copy(res, out_ref, osem)
    out.start()
    gather(6 * CY, 8 * CY, True)

    dims = (((1,), (1,)), ((), ()))

    def scatter(b):
        low, size = BANDS[b]
        ch, cl = split(contrib[pl.ds(low, size), :])
        both = jnp.concatenate([ch, cl], axis=0).astype(BF16)
        none = jnp.zeros((16, PIX), BF16)
        copies = []
        for j in range(4):
            rows = jnp.concatenate(
                [jnp.where(pairs[...] == float(j * 16 + i), both, none) for i in range(16)], axis=0
            )
            got = lax.dot_general(rows, hot[...], dims, preferred_element_type=F32)
            got = got.reshape(4, 4, 16, 2 * CY)
            got = got[:, :, :8] + got[:, :, 8:]
            ds[b, 0, j] = got[..., :CY]
            ds[b, 1, j] = got[..., CY:]
            if j % 2:
                two = pl.ds(j - 1, 2)
                copies.append(send(ds.at[b, 1 - c, two], rc.at[b, two], sibling))
        return copies

    def part(b, fixed):
        idx = [slice(None)] * 3
        for axis, value in fixed.items():
            idx[(1, 0, 2)[axis]] = value
        return ds.at[(b, c) + tuple(idx)]

    sides = ((0, 1), (1, -1), (2, 2))

    def stage_c(b, copies):
        for copy in copies:
            copy.wait_recv()

        def add(i, carry):
            ds[b, c, i] = ds[b, c, i] + rc[b, i]
            return carry

        lax.fori_loop(0, 4, add, 0)
        a1 = ORDERS[b][0]
        return [send(part(b, {a1: at(a1, by)}), r1.at[b, i], dev(a1, by)) for i, by in sides]

    def stage_1(b, copies):
        a1, a2, a3 = ORDERS[b]
        for copy in copies:
            copy.wait_recv()
        here = part(b, {a1: mine[a1]})
        here[...] = here[...] + r1[b, 0] + r1[b, 1] + r1[b, 2]
        return [
            send(part(b, {a1: mine[a1], a2: at(a2, by)}), r2.at[b, i], dev(a2, by))
            for i, by in sides
        ]

    def stage_2(b, copies):
        a1, a2, a3 = ORDERS[b]
        for copy in copies:
            copy.wait_recv()
        here = part(b, {a1: mine[a1], a2: mine[a2]})
        here[...] = here[...] + r2[b, 0] + r2[b, 1] + r2[b, 2]
        return [
            send(part(b, {n: at(n, by if n == a3 else 0) for n in range(3)}),
                 r3.at[b, i], dev(a3, by))
            for i, by in sides
        ]

    def stage_3(b, copies):
        start, size = BANDS[b]
        for copy in copies:
            copy.wait_recv()
        grad_ref[pl.ds(start, size), :] = ds[b, c, y, x, z] + r3[b, 0] + r3[b, 1] + r3[b, 2]

    stages = (scatter, stage_c, stage_1, stage_2, stage_3)
    work = {}
    for b, n in PLAN:
        work[b] = stages[n](b, work[b]) if n else scatter(b)
    out.wait()
    for copy in done:
        copy.wait_send()


def per_device(
    adjoint, concentration, courant_x, courant_y, diffusion, coag_kernel,
    pixel_column, pixel_owner, pixel_slot, pixel_level, pixel_weight,
):
    vmem = pl.BlockSpec(memory_space=pltpu.VMEM)
    smem = pl.BlockSpec(memory_space=pltpu.SMEM)
    hbm = pl.BlockSpec(memory_space=pltpu.HBM)
    field = (SEC, LEV, CX, CY)
    plane = (LEV, CX, CY)

    ints = pltpu.VMEM((1, PIX), jnp.int32)
    return pl.pallas_call(
        kernel,
        out_shape=(
            jax.ShapeDtypeStruct(field, F32),
            jax.ShapeDtypeStruct((SEC, CY), F32),
        ),
        in_specs=[hbm, hbm, hbm, hbm, smem] + [hbm] * 6,
        out_specs=(hbm, vmem),
        scratch_shapes=[
            pltpu.VMEM(field, F32), pltpu.VMEM(field, F32),
            pltpu.VMEM(plane, F32), pltpu.VMEM(plane, F32),
            pltpu.VMEM((SEC, SEC), F32),
            ints, ints, ints, ints, pltpu.VMEM((1, PIX), F32),
            pltpu.VMEM((5,) + plane, F32),
            pltpu.VMEM((SEC, 3 * SEC), BF16), pltpu.VMEM((SEC, 3 * SEC), BF16),
            pltpu.VMEM((2, 2, SEC, 8, CY), F32), pltpu.VMEM((2, SEC, CY), F32),
            pltpu.VMEM((2, 2, SEC, 8, CY), F32), pltpu.VMEM((2, SEC, CY), F32),
            pltpu.VMEM((CX * CY, PIX), BF16), pltpu.VMEM((2 * CY, PIX), BF16),
            pltpu.VMEM((LEV, PIX), F32), pltpu.VMEM((16, PIX), BF16),
            pltpu.VMEM((LEV * 2 * SEC, CX * CY), BF16),
            pltpu.VMEM((SEC, PIX), F32),
            pltpu.VMEM(field, F32),
            pltpu.VMEM((5, 2, 4, 4, 4, 8, CY), F32),
            pltpu.VMEM((5, 4, 4, 4, 8, CY), F32),
            pltpu.VMEM((5, 3, 4, 4, 8, CY), F32),
            pltpu.VMEM((5, 3, 4, 8, CY), F32),
            pltpu.VMEM((5, 3, 8, CY), F32),
            pltpu.SemaphoreType.DMA((10,)),
            pltpu.SemaphoreType.DMA,
            pltpu.SemaphoreType.DMA((61,)),
            pltpu.SemaphoreType.DMA((61,)),
        ],
        compiler_params=pltpu.CompilerParams(
            collective_id=0, has_side_effects=True, vmem_limit_bytes=56 << 20
        ),
    )(
        adjoint, concentration, courant_x, courant_y, diffusion, coag_kernel,
        pixel_column[None, :], pixel_owner[:, 0][None, :], pixel_slot[None, :],
        pixel_level[None, :], pixel_weight[None, :],
    )


def solution(mesh):
    pixels = P(("gx", "gy"))
    placed = (
        P(None, None, "gx", "gy"), P(None, None, "gx", "gy"), P(None, "gx", "gy"),
        P(None, "gx", "gy"), P(), P(), pixels, P(("gx", "gy"), None), pixels, pixels, pixels,
    )
    return jax.shard_map(
        per_device,
        mesh=mesh,
        in_specs=placed,
        out_specs=(P(None, None, "gx", "gy"), P(None, ("gx", "gy"))),
        check_vma=False,
    )
```

time: 76 us -> 60.8 us (0.80)
  Pallas kernels: 71 us -> 55.9 us
    pallas_call x1, Pallas kernels: 71 us -> 55.9 us  [per_device(): pl.pallas_call(kernel, out_shape=(jax.ShapeDtypeStruct(field, F32), jax.S...]
where the time goes in v3:
time: 60.8 us; the launch traced here: 60.7 us
  Pallas kernels  55.9 us (92%)
  local copies, waits for them, and re-layouts  4.15 us (7%)
  between operations  0.65 us (1%)
    pallas_call x1, Pallas kernels, per_device(): pl.pallas_call(kernel, out_shape=(jax.ShapeDtypeStruct(field, F32), jax.S...  55.9 us
    unnamed x4, local copies, waits for them, and re-layouts  4.15 us

profile of v3, /device:TPU:0, one launch (start us, length us, event | category | flops | bytes accessed | tf_op | source)
XLA Modules:
  0.0 60.7 jit_solution(11375062011320139645)
XLA Ops:
  0.6 55.9 %shard_map.122 = (f32[40,16,8,128]{3,2,1,0:T(8,128)}, f32[40,128]{1,0:T(8,128)}) custom-call(f32[40,16,8,128]{3,2,1,0:T(8,128)} %adj_h.1, f32[40,16,8,128]{3,2,1,0:T(8,128)} %conc_h.1, f32[16,8,128]{2,1,0:T(8,128)} %cx_h.1, f32[16,8,128]{2,1,0:T(8,128)} %cy_h.1, f32[16]{0:T(128)} %dif_ref.1, f32[40,40]{1,0:T(8,128)} %ker_h.1, s32[1,2048]{1,0:T(1,128)} %bitcast.5, ...), custom_call_target="tpu_custom_call" | custom-call | tf_op jit(solution)/shard_map/pallas_call | solution.py:356
  56.5 0.0 copy-start
  56.5 3.5 %copy.15 = f32[40,16,8,128]{3,2,1,0:T(8,128)} copy(f32[40,16,8,128]{3,2,1,0:T(8,128)} %get-tuple-element.4) | data formatting | bytes 5242880
  60.1 0.0 copy-done
  60.1 0.6 copy.16
Async XLA Ops:
  56.5 3.6 %copy-start = (f32[40,128]{1,0:T(8,128)S(1)}, f32[40,128]{1,0:T(8,128)}, u32[]{:S(2)}) copy-start(f32[40,128]{1,0:T(8,128)} %get-tuple-element.5) | copy-start | bytes 61444

commit v4 on v3

--- a/solution.py
+++ b/solution.py
@@ -17,9 +17,8 @@
 GROUP_IN = 2
 GROUP_OUT = 4
 PLAN = (
-    (0, 0), (1, 0), (0, 1), (2, 0), (1, 1), (3, 0), (2, 1), (4, 0),
-    (0, 2), (3, 1), (4, 1), (1, 2), (0, 3), (2, 2), (1, 3), (3, 2), (2, 3), (0, 4), (4, 2),
-    (1, 4), (3, 3), (2, 4), (4, 3), (3, 4), (4, 4),
+    (0, 2), (1, 2), (2, 2), (0, 3), (3, 2), (1, 3), (4, 2), (2, 3), (0, 4), (3, 3), (1, 4),
+    (4, 3), (2, 4), (3, 4), (4, 4),
 )
 
 
@@ -41,8 +40,8 @@
     adj_h, conc_h, cx_h, cy_h, dif_ref, ker_h, col_h, own_h, slot_h, lev_h, wgt_h,
     out_ref, grad_ref,
     adj, conc, cx, cy, ker, col, own, slot, lev, wgt,
-    coef, k3, k3t, px, py, rx, ry, cells, hot, prof, pairs, held, contrib, res,
-    ds, rc, r1, r2, r3, lsem, osem, ssem, rsem,
+    coef, k3, k3t, rates, px, py, rx, ry, cells, hot, prof, pairs, held, contrib, contrib2, own2, slot2, pairs2, hot2,
+    ds, r1, r2, r3, lsem, ssem, rsem,
 ):
     gx = lax.axis_index("gx")
     gy = lax.axis_index("gy")
@@ -124,8 +123,6 @@
     fill(0)
     pl.semaphore_wait(barrier, 14)
     sent_x = [[send(px.at[i, 0], rx.at[i, 0], half_peers[i]) for i in range(2)]]
-    fill(1)
-    sent_x.append([send(px.at[i, 1], rx.at[i, 1], half_peers[i]) for i in range(2)])
     lane = lax.broadcasted_iota(jnp.int32, (SEC, CY), 1)
     row = lax.broadcasted_iota(jnp.int32, (SEC, CY), 0)
 
@@ -144,21 +141,51 @@
     low, high = lax.fori_loop(0, LEV, edge, (zero, zero))
     py[0] = low
     py[1] = high
+
     sent_y = [send(py.at[i], ry.at[i], half_peers[2 + i]) for i in range(2)]
-
-    for name in ("ker", "col", "own", "slot", "lev", "wgt", "conc"):
-        loads[name].wait()
+    fill(1)
+    sent_x.append([send(px.at[i, 1], rx.at[i, 1], half_peers[i]) for i in range(2)])
+    loads["own"].wait()
+    loads["slot"].wait()
+    sent_i = [send(own, own2, sibling), send(slot, slot2, sibling)]
+
+    loads["ker"].wait()
+    loads["conc"].wait()
     kh, kl = split(ker[...])
     k3[...] = jnp.concatenate([kh, kh, kl], axis=1).astype(BF16)
     kh, kl = split(ker[...].T)
     k3t[...] = jnp.concatenate([kh, kh, kl], axis=1).astype(BF16)
+    def product(k, v):
+        vh, vl = split(v)
+        v3 = jnp.concatenate([vh, vl, vh], axis=0).astype(BF16)
+        return jnp.dot(k[...], v3, preferred_element_type=F32)
+
+    def rate(it, carry):
+        cc = jnp.concatenate(
+            [conc[:, it * 2 + g, i, :] for g in range(2) for i in range(CX)], axis=1
+        )
+        got = product(k3, cc)
+        for g in range(2):
+            base = pl.multiple_of((it * 2 + g) * SEC, SEC)
+            rates[pl.ds(base, SEC), :] = got[:, g * CX * CY:(g + 1) * CX * CY]
+        return carry
+
+    lax.fori_loop(0, LEV // 2, rate, 0)
+    for name in ("col", "lev", "wgt"):
+        loads[name].wait()
     height = lax.broadcasted_iota(jnp.int32, (LEV, PIX), 0).astype(F32) - lev[...].astype(F32)
     shape = jnp.exp(-height * height / 8.0)
     prof[...] = shape / jnp.sum(shape, axis=0, keepdims=True) * wgt[...]
-    pair = own[...] // 2
-    pairs[...] = jnp.broadcast_to(pair.astype(F32), (16, PIX)).astype(BF16)
-    want = (own[...] - pair * 2) * CY + slot[...]
-
+    def targets(owner, place_in, pair_out, hot_out):
+        cell = owner[...] // 2
+        pair_out[...] = jnp.broadcast_to((cell // 2).astype(F32), (16, PIX)).astype(BF16)
+        want = (cell - cell // 2 * 2) * CY + place_in[...]
+        want = jnp.where(owner[...] - cell * 2 == c, want, -1)
+        for i in range(4):
+            ids = lax.broadcasted_iota(jnp.int32, (64, PIX), 0) + i * 64
+            hot_out[pl.ds(i * 64, 64), :] = jnp.where(ids == want, 1.0, 0.0).astype(BF16)
+
+    targets(own, slot, pairs, hot)
     turned = lax.rem(col[...] + (CX - 1) * CY, CX * CY)
 
     def mark(i, carry):
@@ -168,14 +195,6 @@
         return carry
 
     lax.fori_loop(0, CX * CY // 64, mark, 0)
-    for i in range(4):
-        ids = lax.broadcasted_iota(jnp.int32, (64, PIX), 0) + i * 64
-        hot[pl.ds(i * 64, 64), :] = jnp.where(ids == want, 1.0, 0.0).astype(BF16)
-
-    def product(k, v):
-        vh, vl = split(v)
-        v3 = jnp.concatenate([vh, vl, vh], axis=0).astype(BF16)
-        return jnp.dot(k[...], v3, preferred_element_type=F32)
 
     far_e = jnp.where(gx == 15, 0.0, 1.0)
     far_w = jnp.where(gx == 0, 0.0, 1.0)
@@ -184,7 +203,7 @@
 
     def levels(xs, group, start, stop):
         def step(it, carry):
-            moved, ups, concs = [], [], []
+            moved, ups, concs, turns = [], [], [], []
             for g in range(group):
                 l = it * group + g
                 turn = lax.rem(CY - l * CX, CY)
@@ -213,10 +232,12 @@
                     moved.append(m)
                     ups.append(nxt - m)
                     concs.append(conc[:, l, i, :])
+                    base = pl.multiple_of(l * SEC, SEC)
+                    turns.append(rates[pl.ds(base, SEC), i * CY:(i + 1) * CY])
             m = jnp.concatenate(moved, axis=1)
             up = jnp.concatenate(ups, axis=1)
             cc = jnp.concatenate(concs, axis=1)
-            new = m + up * product(k3, cc) + product(k3t, up * cc)
+            new = m + up * jnp.concatenate(turns, axis=1) + product(k3t, up * cc)
             rh, rl = split(new)
             both = jnp.concatenate([rh, rl], axis=0).astype(BF16)
             n = 0
@@ -226,7 +247,7 @@
                 for i in xs:
                     lanes = slice(n * CY, (n + 1) * CY)
                     spot = (i + CX - 1) % CX * CY
-                    res[:, l, i, :] = new[:, lanes]
+                    out_ref[:, l, i, :] = new[:, lanes]
                     held[at_row, spot:spot + CY] = both[:, lanes]
                     n += 1
             return carry
@@ -254,53 +275,48 @@
         copy.wait_recv()
     levels(range(1, CX - 1), GROUP_IN, 0, LEV // GROUP_IN)
     gather(0, 6 * CY, False)
+    for copy in sent_i:
+        copy.wait_recv()
+    targets(own2, slot2, pairs2, hot2)
     for n in range(2):
         for copy in sent_x[n]:
             copy.wait_recv()
         levels((CX - 1, 0), GROUP_OUT, n * 8 // GROUP_OUT, (n + 1) * 8 // GROUP_OUT)
-    out = pltpu.make_async_copy(res, out_ref, osem)
-    out.start()
     gather(6 * CY, 8 * CY, True)
+    swap = send(contrib, contrib2, sibling)
 
     dims = (((1,), (1,)), ((), ()))
 
-    def scatter(b):
+    def scatter(b, values, pair_in, hot_in, more):
         low, size = BANDS[b]
-        ch, cl = split(contrib[pl.ds(low, size), :])
+        ch, cl = split(values[pl.ds(low, size), :])
         both = jnp.concatenate([ch, cl], axis=0).astype(BF16)
         none = jnp.zeros((16, PIX), BF16)
-        copies = []
-        for j in range(4):
+        for j in range(2):
             rows = jnp.concatenate(
-                [jnp.where(pairs[...] == float(j * 16 + i), both, none) for i in range(16)], axis=0
+                [jnp.where(pair_in[...] == float(j * 16 + i), both, none) for i in range(16)],
+                axis=0,
             )
-            got = lax.dot_general(rows, hot[...], dims, preferred_element_type=F32)
-            got = got.reshape(4, 4, 16, 2 * CY)
-            got = got[:, :, :8] + got[:, :, 8:]
-            ds[b, 0, j] = got[..., :CY]
-            ds[b, 1, j] = got[..., CY:]
-            if j % 2:
-                two = pl.ds(j - 1, 2)
-                copies.append(send(ds.at[b, 1 - c, two], rc.at[b, two], sibling))
-        return copies
+            got = lax.dot_general(rows, hot_in[...], dims, preferred_element_type=F32)
+            for i in range(16):
+                yy, xx, zz = j * 2 + i // 8, i // 2 % 4, i % 2 * 2
+                one = got[i * 16:i * 16 + 8] + got[i * 16 + 8:i * 16 + 16]
+                for k in range(2):
+                    new = one[:, k * CY:(k + 1) * CY]
+                    if more:
+                        new = new + ds[b, yy, xx, zz + k]
+                    ds[b, yy, xx, zz + k] = new
 
     def part(b, fixed):
         idx = [slice(None)] * 3
         for axis, value in fixed.items():
             idx[(1, 0, 2)[axis]] = value
-        return ds.at[(b, c) + tuple(idx)]
+        return ds.at[(b,) + tuple(idx)]
 
     sides = ((0, 1), (1, -1), (2, 2))
 
-    def stage_c(b, copies):
-        for copy in copies:
-            copy.wait_recv()
-
-        def add(i, carry):
-            ds[b, c, i] = ds[b, c, i] + rc[b, i]
-            return carry
-
-        lax.fori_loop(0, 4, add, 0)
+    def stage_c(b):
+        scatter(b, contrib2, pairs2, hot2, True)
         a1 = ORDERS[b][0]
         return [send(part(b, {a1: at(a1, by)}), r1.at[b, i], dev(a1, by)) for i, by in sides]
 
@@ -331,15 +347,29 @@
         start, size = BANDS[b]
         for copy in copies:
             copy.wait_recv()
-        grad_ref[pl.ds(start, size), :] = ds[b, c, y, x, z] + r3[b, 0] + r3[b, 1] + r3[b, 2]
-
-    stages = (scatter, stage_c, stage_1, stage_2, stage_3)
-    work = {}
+        grad_ref[pl.ds(start, size), :] = ds[b, y, x, z] + r3[b, 0] + r3[b, 1] + r3[b, 2]
+
+    for b in range(5):
+        scatter(b, contrib, pairs, hot, False)
+    swap.wait_recv()
+    stages = (None, None, stage_1, stage_2, stage_3)
+    work = [stage_c(b) for b in range(5)]
     for b, n in PLAN:
-        work[b] = stages[n](b, work[b]) if n else scatter(b)
-    out.wait()
+        work[b] = stages[n](b, work[b])
     for copy in done:
         copy.wait_send()
+
+
+def store_kernel(src, grad, dst, grad_dst, sems):
+    copies = [
+        pltpu.make_async_copy(src.at[pl.ds(5 * n, 5)], dst.at[pl.ds(5 * n, 5)], sems.at[n])
+        for n in range(8)
+    ]
+    copies.append(pltpu.make_async_copy(grad, grad_dst, sems.at[8]))
+    for copy in copies:
+        copy.start()
+    for copy in copies:
+        copy.wait()
 
 
 def per_device(
@@ -353,14 +383,14 @@
     plane = (LEV, CX, CY)
 
     ints = pltpu.VMEM((1, PIX), jnp.int32)
-    return pl.pallas_call(
+    got, grad = pl.pallas_call(
         kernel,
         out_shape=(
             jax.ShapeDtypeStruct(field, F32),
             jax.ShapeDtypeStruct((SEC, CY), F32),
         ),
         in_specs=[hbm, hbm, hbm, hbm, smem] + [hbm] * 6,
-        out_specs=(hbm, vmem),
+        out_specs=(vmem, vmem),
         scratch_shapes=[
             pltpu.VMEM(field, F32), pltpu.VMEM(field, F32),
             pltpu.VMEM(plane, F32), pltpu.VMEM(plane, F32),
@@ -368,31 +398,41 @@
             ints, ints, ints, ints, pltpu.VMEM((1, PIX), F32),
             pltpu.VMEM((5,) + plane, F32),
             pltpu.VMEM((SEC, 3 * SEC), BF16), pltpu.VMEM((SEC, 3 * SEC), BF16),
+            pltpu.VMEM((LEV * SEC, CX * CY), F32),
             pltpu.VMEM((2, 2, SEC, 8, CY), F32), pltpu.VMEM((2, SEC, CY), F32),
             pltpu.VMEM((2, 2, SEC, 8, CY), F32), pltpu.VMEM((2, SEC, CY), F32),
             pltpu.VMEM((CX * CY, PIX), BF16), pltpu.VMEM((2 * CY, PIX), BF16),
             pltpu.VMEM((LEV, PIX), F32), pltpu.VMEM((16, PIX), BF16),
             pltpu.VMEM((LEV * 2 * SEC, CX * CY), BF16),
-            pltpu.VMEM((SEC, PIX), F32),
-            pltpu.VMEM(field, F32),
-            pltpu.VMEM((5, 2, 4, 4, 4, 8, CY), F32),
+            pltpu.VMEM((SEC, PIX), F32), pltpu.VMEM((SEC, PIX), F32),
+            ints, ints, pltpu.VMEM((16, PIX), BF16), pltpu.VMEM((2 * CY, PIX), BF16),
             pltpu.VMEM((5, 4, 4, 4, 8, CY), F32),
             pltpu.VMEM((5, 3, 4, 4, 8, CY), F32),
             pltpu.VMEM((5, 3, 4, 8, CY), F32),
             pltpu.VMEM((5, 3, 8, CY), F32),
             pltpu.SemaphoreType.DMA((10,)),
-            pltpu.SemaphoreType.DMA,
-            pltpu.SemaphoreType.DMA((61,)),
-            pltpu.SemaphoreType.DMA((61,)),
+            pltpu.SemaphoreType.DMA((54,)),
+            pltpu.SemaphoreType.DMA((54,)),
         ],
         compiler_params=pltpu.CompilerParams(
-            collective_id=0, has_side_effects=True, vmem_limit_bytes=56 << 20
+            collective_id=0, has_side_effects=True, vmem_limit_bytes=48 << 20
         ),
-    )(
+    )(*(pltpu.with_memory_space_constraint(v, pltpu.HBM) for v in (
         adjoint, concentration, courant_x, courant_y, diffusion, coag_kernel,
         pixel_column[None, :], pixel_owner[:, 0][None, :], pixel_slot[None, :],
         pixel_level[None, :], pixel_weight[None, :],
-    )
+    )))
+    return pl.pallas_call(
+        store_kernel,
+        out_shape=(
+            jax.ShapeDtypeStruct(field, F32),
+            jax.ShapeDtypeStruct((SEC, CY), F32),
+        ),
+        in_specs=[vmem, vmem],
+        out_specs=(hbm, hbm),
+        scratch_shapes=[pltpu.SemaphoreType.DMA((9,))],
+        compiler_params=pltpu.CompilerParams(vmem_limit_bytes=4 << 20),
+    )(got, grad)
 
 
 def solution(mesh):

time: 60.8 us -> 55.4 us (0.911)
  local copies, waits for them, and re-layouts: 4.15 us -> 0 us
  Pallas kernels: 55.9 us -> 54.7 us
    unnamed x4 -> x0, local copies, waits for them, and re-layouts: 4.15 us -> none
    pallas_call x1, Pallas kernels: 55.9 us -> 53.1 us  [per_device(): pl.pallas_call(kernel, out_shape=(jax.ShapeDtypeStruct(field, F32), jax.S...]
    pallas_call x0 -> x1, Pallas kernels: none -> 1.56 us  [per_device(): pl.pallas_call(store_kernel, out_shape=(jax.ShapeDtypeStruct(field, F32),...]
where the time goes in v4:
time: 55.4 us; the launch traced here: 55.3 us
  Pallas kernels  54.7 us (99%)
  between operations  0.64 us (1%)
    pallas_call x1, Pallas kernels, per_device(): pl.pallas_call(kernel, out_shape=(jax.ShapeDtypeStruct(field, F32), jax.S...  53.1 us
    pallas_call x1, Pallas kernels, per_device(): pl.pallas_call(store_kernel, out_shape=(jax.ShapeDtypeStruct(field, F32),...  1.56 us

profile of v4, /device:TPU:0, one launch (start us, length us, event | category | flops | bytes accessed | tf_op | source)
XLA Modules:
  0.0 55.3 jit_solution(10949588387798485144)
XLA Ops:
  0.6 53.1 %shard_map.122 = (f32[40,16,8,128]{3,2,1,0:T(8,128)S(1)}, f32[40,128]{1,0:T(8,128)S(1)}) custom-call(f32[40,16,8,128]{3,2,1,0:T(8,128)} %adj_h.1, f32[40,16,8,128]{3,2,1,0:T(8,128)} %conc_h.1, f32[16,8,128]{2,1,0:T(8,128)} %cx_h.1, f32[16,8,128]{2,1,0:T(8,128)} %cy_h.1, f32[16]{0:T(128)} %dif_ref.1, f32[40,40]{1,0:T(8,128)} %ker_h.1, s32[1,2048]{1,0:T(1,128)} %bitcast.5, ...), custom_call_target="tpu_custom_call" | custom-call | tf_op jit(solution)/shard_map/pallas_call | solution.py:386
  53.7 1.6 %shard_map.123 = (f32[40,16,8,128]{3,2,1,0:T(8,128)}, f32[40,128]{1,0:T(8,128)}) custom-call(f32[40,16,8,128]{3,2,1,0:T(8,128)S(1)} %get-tuple-element.4.src, f32[40,128]{1,0:T(8,128)S(1)} %get-tuple-element.5.grad), custom_call_target="tpu_custom_call" | custom-call | tf_op jit(solution)/shard_map/pallas_call | solution.py:425

commit v5 on v4

--- a/solution.py
+++ b/solution.py
@@ -17,8 +17,7 @@
 GROUP_IN = 2
 GROUP_OUT = 4
 PLAN = (
-    (0, 2), (1, 2), (2, 2), (0, 3), (3, 2), (1, 3), (4, 2), (2, 3), (0, 4), (3, 3), (1, 4),
-    (4, 3), (2, 4), (3, 4), (4, 4),
+    (0, 1), (1, 1), (2, 1), (3, 1), (4, 1), (0, 2), (1, 2), (2, 2), (3, 2), (4, 2),
 )
 
 
@@ -41,7 +40,7 @@
     out_ref, grad_ref,
     adj, conc, cx, cy, ker, col, own, slot, lev, wgt,
     coef, k3, k3t, rates, px, py, rx, ry, cells, hot, prof, pairs, held, contrib, contrib2, own2, slot2, pairs2, hot2,
-    ds, r1, r2, r3, lsem, ssem, rsem,
+    ds, r1, r2, lsem, ssem, rsem, fsem, gsem,
 ):
     gx = lax.axis_index("gx")
     gy = lax.axis_index("gy")
@@ -63,14 +62,10 @@
         zz = at(2, by) if axis == 2 else z
         return (yy * 4 + xx, zz * 2 + c)
 
+    def spot(by):
+        return (at(1, by[1]) * 4 + at(0, by[0]), at(2, by[2]) * 2 + c)
+
     sibling = (gx, z * 2 + 1 - c)
-    barrier = pltpu.get_barrier_semaphore()
-    for peer in half_peers:
-        pl.semaphore_signal(barrier, 1, device_id=peer, device_id_type=MESH)
-    pl.semaphore_signal(barrier, 1, device_id=sibling, device_id_type=MESH)
-    for axis in range(3):
-        for by in (1, -1, 2):
-            pl.semaphore_signal(barrier, 1, device_id=dev(axis, by), device_id_type=MESH)
     loads = {}
     for i, (name, src, dst) in enumerate((
         ("cx", cx_h, cx), ("cy", cy_h, cy), ("adj", adj_h, adj), ("conc", conc_h, conc),
@@ -79,6 +74,17 @@
     )):
         loads[name] = pltpu.make_async_copy(src, dst, lsem.at[i])
         loads[name].start()
+    barrier = pltpu.get_barrier_semaphore()
+    for peer in half_peers:
+        pl.semaphore_signal(barrier, 1, device_id=peer, device_id_type=MESH)
+    pl.semaphore_signal(barrier, 1, device_id=sibling, device_id_type=MESH)
+    for dx in range(4):
+        for dy in range(4):
+            for dz in range(4):
+                if 0 < (dx > 0) + (dy > 0) + (dz > 0) < 3:
+                    pl.semaphore_signal(
+                        barrier, 1, device_id=spot((dx, dy, dz)), device_id_type=MESH
+                    )
     count = [0]
     done = []
 
@@ -121,8 +127,7 @@
         lax.fori_loop(0, SEC, one, 0, unroll=4)
 
     fill(0)
-    pl.semaphore_wait(barrier, 14)
-    sent_x = [[send(px.at[i, 0], rx.at[i, 0], half_peers[i]) for i in range(2)]]
+    fill(1)
     lane = lax.broadcasted_iota(jnp.int32, (SEC, CY), 1)
     row = lax.broadcasted_iota(jnp.int32, (SEC, CY), 0)
 
@@ -142,9 +147,11 @@
     py[0] = low
     py[1] = high
 
+    pl.semaphore_wait(barrier, 41)
     sent_y = [send(py.at[i], ry.at[i], half_peers[2 + i]) for i in range(2)]
-    fill(1)
-    sent_x.append([send(px.at[i, 1], rx.at[i, 1], half_peers[i]) for i in range(2)])
+    sent_x = [
+        [send(px.at[i, n], rx.at[i, n], half_peers[i]) for i in range(2)] for n in range(2)
+    ]
     loads["own"].wait()
     loads["slot"].wait()
     sent_i = [send(own, own2, sibling), send(slot, slot2, sibling)]
@@ -326,38 +333,42 @@
             copy.wait_recv()
         here = part(b, {a1: mine[a1]})
         here[...] = here[...] + r1[b, 0] + r1[b, 1] + r1[b, 2]
-        return [
-            send(part(b, {a1: mine[a1], a2: at(a2, by)}), r2.at[b, i], dev(a2, by))
-            for i, by in sides
-        ]
-
-    def stage_2(b, copies):
-        a1, a2, a3 = ORDERS[b]
-        for copy in copies:
-            copy.wait_recv()
-        here = part(b, {a1: mine[a1], a2: mine[a2]})
-        here[...] = here[...] + r2[b, 0] + r2[b, 1] + r2[b, 2]
-        return [
-            send(part(b, {n: at(n, by if n == a3 else 0) for n in range(3)}),
-                 r3.at[b, i], dev(a3, by))
-            for i, by in sides
-        ]
-
-    def stage_3(b, copies):
+
+        def one(i, carry):
+            by = [0, 0, 0]
+            by[a2] = i // 4
+            by[a3] = lax.rem(i, 4)
+            pltpu.make_async_remote_copy(
+                ds.at[b, at(1, by[1]), at(0, by[0]), at(2, by[2])], r2.at[b, i],
+                fsem.at[b], gsem.at[b], device_id=spot(by), device_id_type=MESH,
+            ).start()
+            return carry
+
+        lax.fori_loop(1, 16, one, 0)
+
+    def stage_2(b):
         start, size = BANDS[b]
-        for copy in copies:
-            copy.wait_recv()
-        grad_ref[pl.ds(start, size), :] = ds[b, y, x, z] + r3[b, 0] + r3[b, 1] + r3[b, 2]
+        rest = r2.at[b, pl.ds(1, 15)]
+        pltpu.make_async_copy(rest, rest, gsem.at[b]).wait()
+        total = ds[b, y, x, z]
+        for i in range(1, 16):
+            total = total + r2[b, i]
+        grad_ref[pl.ds(start, size), :] = total
 
     for b in range(5):
         scatter(b, contrib, pairs, hot, False)
     swap.wait_recv()
-    stages = (None, None, stage_1, stage_2, stage_3)
     work = [stage_c(b) for b in range(5)]
     for b, n in PLAN:
-        work[b] = stages[n](b, work[b])
+        if n == 1:
+            stage_1(b, work[b])
+        else:
+            stage_2(b)
     for copy in done:
         copy.wait_send()
+    for b in range(5):
+        rest = r2.at[b, pl.ds(1, 15)]
+        pltpu.make_async_copy(rest, rest, fsem.at[b]).wait()
 
 
 def store_kernel(src, grad, dst, grad_dst, sems):
@@ -408,11 +419,12 @@
             ints, ints, pltpu.VMEM((16, PIX), BF16), pltpu.VMEM((2 * CY, PIX), BF16),
             pltpu.VMEM((5, 4, 4, 4, 8, CY), F32),
             pltpu.VMEM((5, 3, 4, 4, 8, CY), F32),
-            pltpu.VMEM((5, 3, 4, 8, CY), F32),
-            pltpu.VMEM((5, 3, 8, CY), F32),
+            pltpu.VMEM((5, 16, 8, CY), F32),
             pltpu.SemaphoreType.DMA((10,)),
-            pltpu.SemaphoreType.DMA((54,)),
-            pltpu.SemaphoreType.DMA((54,)),
+            pltpu.SemaphoreType.DMA((24,)),
+            pltpu.SemaphoreType.DMA((24,)),
+            pltpu.SemaphoreType.DMA((5,)),
+            pltpu.SemaphoreType.DMA((5,)),
         ],
         compiler_params=pltpu.CompilerParams(
             collective_id=0, has_side_effects=True, vmem_limit_bytes=48 << 20

time: 55.4 us -> 52.1 us (0.940)
  Pallas kernels: 54.7 us -> 51.3 us
    pallas_call x1, Pallas kernels: 53.1 us -> 49.7 us  [per_device(): pl.pallas_call(kernel, out_shape=(jax.ShapeDtypeStruct(field, F32), jax.S...]
where the time goes in v5:
time: 52.1 us; the launch traced here: 51.9 us
  Pallas kernels  51.3 us (98%)
  between operations  0.64 us (1%)
    pallas_call x1, Pallas kernels, per_device(): pl.pallas_call(kernel, out_shape=(jax.ShapeDtypeStruct(field, F32), jax.S...  49.7 us
    pallas_call x1, Pallas kernels, per_device(): pl.pallas_call(store_kernel, out_shape=(jax.ShapeDtypeStruct(field, F32),...  1.56 us

profile of v5, /device:TPU:0, one launch (start us, length us, event | category | flops | bytes accessed | tf_op | source)
XLA Modules:
  0.0 51.9 jit_solution(3463837000702098668)
XLA Ops:
  0.6 49.7 %shard_map.122 = (f32[40,16,8,128]{3,2,1,0:T(8,128)S(1)}, f32[40,128]{1,0:T(8,128)S(1)}) custom-call(f32[40,16,8,128]{3,2,1,0:T(8,128)} %adj_h.1, f32[40,16,8,128]{3,2,1,0:T(8,128)} %conc_h.1, f32[16,8,128]{2,1,0:T(8,128)} %cx_h.1, f32[16,8,128]{2,1,0:T(8,128)} %cy_h.1, f32[16]{0:T(128)} %dif_ref.1, f32[40,40]{1,0:T(8,128)} %ker_h.1, s32[1,2048]{1,0:T(1,128)} %bitcast.5, ...), custom_call_target="tpu_custom_call" | custom-call | tf_op jit(solution)/shard_map/pallas_call | solution.py:397
  50.4 1.6 %shard_map.123 = (f32[40,16,8,128]{3,2,1,0:T(8,128)}, f32[40,128]{1,0:T(8,128)}) custom-call(f32[40,16,8,128]{3,2,1,0:T(8,128)S(1)} %get-tuple-element.4.src, f32[40,128]{1,0:T(8,128)S(1)} %get-tuple-element.5.grad), custom_call_target="tpu_custom_call" | custom-call | tf_op jit(solution)/shard_map/pallas_call | solution.py:437

commit v6 on v5

--- a/solution.py
+++ b/solution.py
@@ -39,7 +39,7 @@
     adj_h, conc_h, cx_h, cy_h, dif_ref, ker_h, col_h, own_h, slot_h, lev_h, wgt_h,
     out_ref, grad_ref,
     adj, conc, cx, cy, ker, col, own, slot, lev, wgt,
-    coef, k3, k3t, rates, px, py, rx, ry, cells, hot, prof, pairs, held, contrib, contrib2, own2, slot2, pairs2, hot2,
+    coef, k3, k3t, px, py, rx, ry, cells, hot, prof, pairs, held, contrib, contrib2, own2, slot2, pairs2, hot2,
     ds, r1, r2, lsem, ssem, rsem, fsem, gsem,
 ):
     gx = lax.axis_index("gx")
@@ -167,17 +167,6 @@
         v3 = jnp.concatenate([vh, vl, vh], axis=0).astype(BF16)
         return jnp.dot(k[...], v3, preferred_element_type=F32)
 
-    def rate(it, carry):
-        cc = jnp.concatenate(
-            [conc[:, it * 2 + g, i, :] for g in range(2) for i in range(CX)], axis=1
-        )
-        got = product(k3, cc)
-        for g in range(2):
-            base = pl.multiple_of((it * 2 + g) * SEC, SEC)
-            rates[pl.ds(base, SEC), :] = got[:, g * CX * CY:(g + 1) * CX * CY]
-        return carry
-
-    lax.fori_loop(0, LEV // 2, rate, 0)
     for name in ("col", "lev", "wgt"):
         loads[name].wait()
     height = lax.broadcasted_iota(jnp.int32, (LEV, PIX), 0).astype(F32) - lev[...].astype(F32)
@@ -210,7 +199,7 @@
 
     def levels(xs, group, start, stop):
         def step(it, carry):
-            moved, ups, concs, turns = [], [], [], []
+            moved, ups, concs = [], [], []
             for g in range(group):
                 l = it * group + g
                 turn = lax.rem(CY - l * CX, CY)
@@ -239,12 +228,10 @@
                     moved.append(m)
                     ups.append(nxt - m)
                     concs.append(conc[:, l, i, :])
-                    base = pl.multiple_of(l * SEC, SEC)
-                    turns.append(rates[pl.ds(base, SEC), i * CY:(i + 1) * CY])
             m = jnp.concatenate(moved, axis=1)
             up = jnp.concatenate(ups, axis=1)
             cc = jnp.concatenate(concs, axis=1)
-            new = m + up * jnp.concatenate(turns, axis=1) + product(k3t, up * cc)
+            new = m + up * product(k3, cc) + product(k3t, up * cc)
             rh, rl = split(new)
             both = jnp.concatenate([rh, rl], axis=0).astype(BF16)
             n = 0
@@ -409,7 +396,6 @@
             ints, ints, ints, ints, pltpu.VMEM((1, PIX), F32),
             pltpu.VMEM((5,) + plane, F32),
             pltpu.VMEM((SEC, 3 * SEC), BF16), pltpu.VMEM((SEC, 3 * SEC), BF16),
-            pltpu.VMEM((LEV * SEC, CX * CY), F32),
             pltpu.VMEM((2, 2, SEC, 8, CY), F32), pltpu.VMEM((2, SEC, CY), F32),
             pltpu.VMEM((2, 2, SEC, 8, CY), F32), pltpu.VMEM((2, SEC, CY), F32),
             pltpu.VMEM((CX * CY, PIX), BF16), pltpu.VMEM((2 * CY, PIX), BF16),

time: 52.1 us -> 50.7 us (0.973)
  the two profiles are of different devices: /device:TPU:0 before, /device:TPU:1 now
where the time goes in v6:
time: 50.7 us; the launch traced here: 50.6 us
  Pallas kernels  50 us (99%)
  between operations  0.64 us (1%)
    pallas_call x1, Pallas kernels, per_device(): pl.pallas_call(kernel, out_shape=(jax.ShapeDtypeStruct(field, F32), jax.S...  48.4 us
    pallas_call x1, Pallas kernels, per_device(): pl.pallas_call(store_kernel, out_shape=(jax.ShapeDtypeStruct(field, F32),...  1.56 us

profile of v6, /device:TPU:1, one launch (start us, length us, event | category | flops | bytes accessed | tf_op | source)
XLA Modules:
  0.0 50.6 jit_solution(2514361051782016052)
XLA Ops:
  0.6 48.4 %shard_map.122 = (f32[40,16,8,128]{3,2,1,0:T(8,128)S(1)}, f32[40,128]{1,0:T(8,128)S(1)}) custom-call(f32[40,16,8,128]{3,2,1,0:T(8,128)} %adj_h.1, f32[40,16,8,128]{3,2,1,0:T(8,128)} %conc_h.1, f32[16,8,128]{2,1,0:T(8,128)} %cx_h.1, f32[16,8,128]{2,1,0:T(8,128)} %cy_h.1, f32[16]{0:T(128)} %dif_ref.1, f32[40,40]{1,0:T(8,128)} %ker_h.1, s32[1,2048]{1,0:T(1,128)} %bitcast.5, ...), custom_call_target="tpu_custom_call" | custom-call | tf_op jit(solution)/shard_map/pallas_call | solution.py:384
  49.0 1.6 %shard_map.123 = (f32[40,16,8,128]{3,2,1,0:T(8,128)}, f32[40,128]{1,0:T(8,128)}) custom-call(f32[40,16,8,128]{3,2,1,0:T(8,128)S(1)} %get-tuple-element.4.src, f32[40,128]{1,0:T(8,128)S(1)} %get-tuple-element.5.grad), custom_call_target="tpu_custom_call" | custom-call | tf_op jit(solution)/shard_map/pallas_call | solution.py:423

commit v7 on v6

--- a/solution.py
+++ b/solution.py
@@ -15,7 +15,7 @@
 BANDS = tuple((8 * b, 8) for b in range(5))
 ORDERS = ((0, 1, 2), (1, 2, 0), (2, 0, 1), (0, 1, 2), (1, 2, 0))
 GROUP_IN = 2
-GROUP_OUT = 4
+GROUP_OUT = 8
 PLAN = (
     (0, 1), (1, 1), (2, 1), (3, 1), (4, 1), (0, 2), (1, 2), (2, 2), (3, 2), (4, 2),
 )
@@ -307,7 +307,7 @@
             idx[(1, 0, 2)[axis]] = value
         return ds.at[(b,) + tuple(idx)]
 
-    sides = ((0, 1), (1, -1), (2, 2))
+    sides = ((2, 2), (0, 1), (1, -1))
 
     def stage_c(b):
         scatter(b, contrib2, pairs2, hot2, True)

time: 50.7 us -> 50.3 us (level)
  no operation moved by 1% of the time
where the time goes in v7:
time: 50.3 us; the launch traced here: 50.2 us
  Pallas kernels  49.6 us (99%)
  between operations  0.64 us (1%)
    pallas_call x1, Pallas kernels, per_device(): pl.pallas_call(kernel, out_shape=(jax.ShapeDtypeStruct(field, F32), jax.S...  48 us
    pallas_call x1, Pallas kernels, per_device(): pl.pallas_call(store_kernel, out_shape=(jax.ShapeDtypeStruct(field, F32),...  1.56 us

profile of v7, /device:TPU:1, one launch (start us, length us, event | category | flops | bytes accessed | tf_op | source)
XLA Modules:
  0.0 50.2 jit_solution(7163732243993531903)
XLA Ops:
  0.6 48.0 %shard_map.122 = (f32[40,16,8,128]{3,2,1,0:T(8,128)S(1)}, f32[40,128]{1,0:T(8,128)S(1)}) custom-call(f32[40,16,8,128]{3,2,1,0:T(8,128)} %adj_h.1, f32[40,16,8,128]{3,2,1,0:T(8,128)} %conc_h.1, f32[16,8,128]{2,1,0:T(8,128)} %cx_h.1, f32[16,8,128]{2,1,0:T(8,128)} %cy_h.1, f32[16]{0:T(128)} %dif_ref.1, f32[40,40]{1,0:T(8,128)} %ker_h.1, s32[1,2048]{1,0:T(1,128)} %bitcast.5, ...), custom_call_target="tpu_custom_call" | custom-call | tf_op jit(solution)/shard_map/pallas_call | solution.py:384
  48.6 1.6 %shard_map.123 = (f32[40,16,8,128]{3,2,1,0:T(8,128)}, f32[40,128]{1,0:T(8,128)}) custom-call(f32[40,16,8,128]{3,2,1,0:T(8,128)S(1)} %get-tuple-element.4.src, f32[40,128]{1,0:T(8,128)S(1)} %get-tuple-element.5.grad), custom_call_target="tpu_custom_call" | custom-call | tf_op jit(solution)/shard_map/pallas_call | solution.py:423
